TPU v7x, 32 devices: a whole 2x2x4 slice. The times are simulated.
32 devices in a mesh: sample: 2 (over x), row: 16 (over z, y, core).
Axes of the slice: x: 2, y: 2, z: 4, core: 2. Of those that a mesh axis runs over, the one named last changes fastest.
Arguments:
- atom_single: bfloat16 [16384, 128], P(('sample', 'row')), parts along dimension 0, may hold values from -6 to 6
- atom_count: int32 [16], replicated, may hold values from 128 to 512, as said below
- atom_token: int32 [8192], P('row'), may hold values from 0 to 63, as said below
- atom_bias: bfloat16 [256, 4, 32, 128], P('row'), may hold values from -4 to 236
- token_single: bfloat16 [2048, 768], P(('sample', 'row')), parts along dimension 0, may hold values from -6 to 6
- token_bias: bfloat16 [16, 1024, 1024], P(None, 'row'), may hold values from -4 to 236
- atom_gain: float32 [128], replicated, may hold values from 0.25 to 1.75
- atom_qkvg: bfloat16 [128, 512], replicated, may hold values from -0.5 to 0.5
- atom_proj: bfloat16 [128, 128], replicated, may hold values from -0.5 to 0.5
- atom_to_token: bfloat16 [128, 768], replicated, may hold values from -0.5 to 0.5
- token_gain: float32 [768], replicated, may hold values from 0.25 to 1.75
- token_qg: bfloat16 [768, 1536], replicated, may hold values from -0.21875 to 0.21875
- token_kv: bfloat16 [768, 1536], replicated, may hold values from -0.21875 to 0.21875
- token_proj: bfloat16 [768, 768], replicated, may hold values from -0.21875 to 0.21875
- token_to_atom: bfloat16 [768, 128], replicated, may hold values from -0.21875 to 0.21875
Outputs:
- atom_out: bfloat16 [16384, 128], P(('sample', 'row')), parts along dimension 0
- token_out: bfloat16 [2048, 768], P(('sample', 'row')), parts along dimension 0
There are 2 independent parts, one for each index of `sample`. A program takes and returns all parts, laid end to end along the dimension named above; an argument that names none is the same for every part. Nothing has to cross between parts.
Inputs may be any that keep to these rules, and one draw needn't show every extreme that they name: `atom_count`: entry b counts the live slots of atoms b * 512 to (b + 1) * 512 - 1, which are the first ones of that block; some block has exactly 512 and another exactly 128. `atom_token`: within a block of 512 slots the live slots' values never fall and each of the 64 values occurs in at least one live slot; slots that are not live hold 0.
All inputs are finite; a program needn't handle non-finite values.
Results may differ from a plain program's by a relative error of at most 0.0051.
Values may be sent and summed in bfloat16 or wider, within the bound.
No kernel may reach another device: no remote copies, remote signals or barrier semaphores. Data moves between devices by JAX's collectives and lax.ppermute only.
A program may use at most 128 MiB of HBM per device.

v0:
```python
import jax
import jax.numpy as jnp
from jax import lax
from jax.experimental import pallas as pl
from jax.experimental.pallas import tpu as pltpu
from jax.sharding import PartitionSpec as P


TW = 768
TH = 16
AW = 128
AH = 4
WQ = 32
WK = 128
LEFT_RIM = 48
RIGHT_RIM = 80
AD = AW // AH
TD = TW // TH

EPSILON = 1e-05
MASKED = -1000000000.0
F32 = jnp.float32
BF16 = jnp.bfloat16
VMEM = pltpu.VMEM
SMEM = pltpu.SMEM


def mm(a, b):
    return lax.dot_general(a, b, (((1,), (0,)), ((), ())), preferred_element_type=F32)


def mm_nt(a, b):
    return lax.dot_general(a, b, (((1,), (1,)), ((), ())), preferred_element_type=F32)


def mm_tn(a, b):
    return lax.dot_general(a, b, (((0,), (0,)), ((), ())), preferred_element_type=F32)


def normalise(values, gain):
    average = jnp.mean(values, axis=-1, keepdims=True)
    centred = values - average
    spread = jnp.mean(centred * centred, axis=-1, keepdims=True)
    return (centred * lax.rsqrt(spread + EPSILON) * gain).astype(BF16)


def sigmoid(values):
    return 1.0 / (1.0 + jnp.exp(-values))


def membership(tok, count, tokens):
    atoms = tok.shape[1]
    slot = lax.broadcasted_iota(jnp.int32, (tokens, atoms), 1)
    name = lax.broadcasted_iota(jnp.int32, (tokens, atoms), 0)
    return (tok == name) & (slot < count)


def attend_window(q, k, v, bias, first, low, high):
    lane = lax.broadcasted_iota(jnp.int32, (WQ, AW), 1) // AD
    spread_q = jnp.concatenate(
        [jnp.where(lane == h, q, jnp.zeros_like(q)) for h in range(AH)], axis=0
    )
    scores = mm_nt(spread_q, k) * AD ** (-0.5)
    scores = scores + bias.reshape(AH * WQ, WK).astype(F32)
    p = lax.broadcasted_iota(jnp.int32, (1, WK), 1) + first
    scores = jnp.where((p >= low) & (p < high), scores, MASKED)
    raised = jnp.exp(scores - jnp.max(scores, axis=-1, keepdims=True))
    both = mm(raised.astype(BF16), jnp.concatenate([v, jnp.ones_like(v)], axis=1))
    mixed = both[:, :AW] / both[:, AW:]
    out = jnp.zeros((WQ, AW), F32)
    for h in range(AH):
        out = jnp.where(lane == h, mixed[WQ * h : WQ * (h + 1)], out)
    return out


def early_body(
    info, x_hbm, bias_hbm, gain, qkvg_hbm, q_out, kv_out, gate_out, att_out, x, bias, qkvg, sems
):
    row = lax.axis_index("row")
    count = info[row]
    atoms = x.shape[0]
    half = atoms // WQ // 2
    copies = [
        pltpu.make_async_copy(x_hbm, x, sems.at[0]),
        pltpu.make_async_copy(qkvg_hbm, qkvg, sems.at[1]),
        pltpu.make_async_copy(bias_hbm.at[:half], bias.at[:half], sems.at[2]),
        pltpu.make_async_copy(bias_hbm.at[half:], bias.at[half:], sems.at[3]),
    ]
    for copy in copies:
        copy.start()
    copies[0].wait()
    normed = normalise(x[...].astype(F32), gain[...])
    copies[1].wait()
    parts = mm(normed, qkvg[...]).astype(BF16)
    q_out[...] = parts[:, :AW]
    gate_out[...] = parts[:, 3 * AW :]
    kv_out[0:LEFT_RIM, :] = jnp.zeros((LEFT_RIM, 2 * AW), BF16)
    kv_out[LEFT_RIM : LEFT_RIM + atoms, :] = parts[:, AW : 3 * AW]
    kv_out[LEFT_RIM + atoms :, :] = jnp.zeros((RIGHT_RIM, 2 * AW), BF16)
    for w in range(atoms // WQ):
        if w % half == 0:
            copies[2 + w // half].wait()
        rows = slice(WQ * w, WQ * w + WK)
        att_out[WQ * w : WQ * (w + 1), :] = attend_window(
            q_out[WQ * w : WQ * (w + 1), :], kv_out[rows, :AW], kv_out[rows, AW:],
            bias[w], WQ * w - LEFT_RIM, 0, count,
        )


def late_body(
    info, near, far, q, kv_in, gate_in, att_in, tok, gain, tgain, bias, qkvg_hbm, x_hbm, proj_hbm,
    lift_hbm, tsingle_hbm, normed_out, hidden_out, mid_out, kv, att, some, qkvg, x, proj, lift,
    tsingle, sems,
):
    row = lax.axis_index("row")
    width = lax.axis_size("row")
    count = info[row]
    atoms = x.shape[0]
    tokens = tsingle.shape[0]
    last = (count - 1) // WQ
    head = pltpu.make_async_copy(bias.at[0:2], some.at[0:2], sems.at[0])
    head.start()
    tail = pltpu.make_async_copy(bias.at[pl.ds(last - 2, 3)], some.at[2:5], sems.at[1])
    tail.start()
    copies = [
        pltpu.make_async_copy(source, target, sems.at[2 + i])
        for i, (source, target) in enumerate(
            [
                (qkvg_hbm.at[:, AW : 3 * AW], qkvg), (x_hbm, x), (proj_hbm, proj),
                (lift_hbm, lift), (tsingle_hbm, tsingle),
            ]
        )
    ]
    for copy in copies:
        copy.start()
    odd = row % 2 == 1
    previous = jnp.where(odd, near[...], far[...])
    following = jnp.where(odd, far[0:RIGHT_RIM, :], near[0:RIGHT_RIM, :])
    before_count = info[jnp.maximum(row - 1, 0)]
    r = lax.broadcasted_iota(jnp.int32, (LEFT_RIM, atoms), 0) + (before_count - LEFT_RIM)
    pick = r == lax.broadcasted_iota(jnp.int32, (LEFT_RIM, atoms), 1)
    before = mm(jnp.where(pick, 1.0, 0.0).astype(BF16), previous)
    rims = jnp.concatenate([before, following.astype(F32)], axis=0)
    rims = normalise(rims, gain[...])
    copies[0].wait()
    rim_kv = mm(rims, qkvg[...]).astype(BF16)
    after_kv = rim_kv[LEFT_RIM:]
    kv[...] = kv_in[...]
    kv[0:LEFT_RIM, :] = rim_kv[:LEFT_RIM]
    att[...] = att_in[...]
    low = jnp.where(row == 0, 0, -4 * atoms)
    high = jnp.where(row == width - 1, count, 4 * atoms)
    region = 2 * WQ + WK
    start = pl.multiple_of((last - 2) * WQ, WQ)
    r = lax.broadcasted_iota(jnp.int32, (region, RIGHT_RIM), 0) + (start - LEFT_RIM - count)
    pick = r == lax.broadcasted_iota(jnp.int32, (region, RIGHT_RIM), 1)
    moved = mm(jnp.where(pick, 1.0, 0.0).astype(BF16), after_kv)
    r = lax.broadcasted_iota(jnp.int32, (region, 2 * AW), 0) + (start - LEFT_RIM - count)
    local = kv[pl.ds(start, region), :].astype(F32)
    local = jnp.where((r >= 0) & (r < RIGHT_RIM), moved, local).astype(BF16)
    head.wait()
    tail.wait()
    for w in range(2):
        rows = slice(WQ * w, WQ * w + WK)
        att[WQ * w : WQ * (w + 1), :] = attend_window(
            q[WQ * w : WQ * (w + 1), :], kv[rows, :AW], kv[rows, AW:], some[w],
            WQ * w - LEFT_RIM, low, high,
        )
    for w in range(3):
        at = pl.multiple_of(start + WQ * w, WQ)
        rows = slice(WQ * w, WQ * w + WK)
        att[pl.ds(at, WQ), :] = attend_window(
            q[pl.ds(at, WQ), :], local[rows, :AW], local[rows, AW:], some[2 + w],
            at - LEFT_RIM, low, high,
        )
    gated = (att[...] * sigmoid(gate_in[...].astype(F32))).astype(BF16)
    copies[1].wait()
    copies[2].wait()
    mid = (x[...].astype(F32) + mm(gated, proj[...])).astype(BF16)
    mid_out[...] = mid
    copies[3].wait()
    lifted = jnp.maximum(mm(mid, lift[...]), 0.0).astype(BF16)
    member = jnp.where(membership(tok[...], count, tokens), 1.0, 0.0)
    summed = mm(member.astype(BF16), lifted)
    counts = jnp.sum(member, axis=1, keepdims=True)
    copies[4].wait()
    hidden = tsingle[...].astype(F32) + summed / counts
    hidden_out[...] = hidden
    normed_out[...] = normalise(hidden, tgain[...])


def head_windows():
    windows = []
    h = 0
    while h < TH:
        first = h * TD // 128 * 128
        first = min(first, TW - 256)
        heads = []
        while h < TH and (h + 1) * TD <= first + 256:
            heads.append(h)
            h += 1
        windows.append((first, heads))
    return windows


def query_body(info, normed, tok, qg, out, member_out, normed_out):
    tokens = normed.shape[0]
    member = membership(tok[...], info[lax.axis_index("row")], tokens)
    r = lax.broadcasted_iota(jnp.int32, (tokens, 3 * tokens), 0)
    c = lax.broadcasted_iota(jnp.int32, (tokens, 3 * tokens), 1)
    same = (c == r) | (c == r + tokens) | (c == r + 2 * tokens)
    one = jnp.where(member, 1.0, 0.0).astype(BF16)
    member_out[...] = mm_tn(one, jnp.where(same, 1.0, 0.0).astype(BF16)).astype(BF16)
    normed_out[...] = normed[...]
    out[...] = mm(normed[...], qg[...]).astype(BF16)


def token_body(offsets, begins, ends, *refs):
    number = len(offsets)
    own, oth, refs = refs[:number], refs[number : 2 * number], refs[2 * number :]
    query_gate, kv, bias, *refs = refs
    if not begins:
        st_in, acc_in, *refs = refs
    if ends:
        info, hidden_in, mid, member, proj_hbm, down, atom_out, token_out, *refs = refs
        xs, kvs, qs, proj, sems = refs
    else:
        st_out, acc_out, *refs = refs
        xs, kvs, qs = refs
    row = lax.axis_index("row")
    chip, core = row // 2, row % 2
    tokens = own[0].shape[0]
    pair = 2 * tokens
    keys = number * pair
    if ends:
        fetch = pltpu.make_async_copy(proj_hbm, proj, sems.at[0])
        fetch.start()
    for j in range(number):
        at = pl.multiple_of(j * pair + core * tokens, tokens)
        xs[pl.ds(at, tokens), :] = own[j][...]
        at = pl.multiple_of(j * pair + (1 - core) * tokens, tokens)
        xs[pl.ds(at, tokens), :] = oth[j][...]
    column = lax.broadcasted_iota(jnp.int32, (tokens, 256), 1)
    windows = head_windows()
    for first, heads in windows:
        q = query_gate[:, first : first + 256]
        for h in heads:
            keep = (column >= h * TD - first) & (column < (h + 1) * TD - first)
            qs[h * tokens : (h + 1) * tokens, :] = jnp.where(keep, q, jnp.zeros_like(q))
    kvs[...] = mm(xs[...], kv[...]).astype(BF16)
    places = [pl.multiple_of((chip ^ offset) * pair, pair) for offset in offsets]
    pieces = [jnp.zeros((tokens, 128), F32) for _ in range(TW // 128)]
    tile_column = lax.broadcasted_iota(jnp.int32, (tokens, 128), 1)
    key_column = lax.broadcasted_iota(jnp.int32, (keys, 256), 1)
    for first, heads in windows:
        rows = slice(heads[0] * tokens, (heads[-1] + 1) * tokens)
        used = (heads[0] * TD - first, (heads[-1] + 1) * TD - first)
        spare = 255 if used[1] < 256 else 0
        scores = mm_nt(qs[rows, :], kvs[:, first : first + 256]) * TD ** (-0.5)
        tile = jnp.concatenate(
            [
                bias[heads[0] : heads[-1] + 1, :, pl.ds(at, pair)].reshape(-1, pair)
                for at in places
            ],
            axis=1,
        )
        scores = scores + tile.astype(F32)
        best = jnp.broadcast_to(jnp.max(scores, axis=-1, keepdims=True), (scores.shape[0], 128))
        if not begins:
            best = jnp.maximum(best, st_in[rows, :])
        raised = jnp.concatenate(
            [
                jnp.exp(scores[:, i : i + 128] - best).astype(BF16)
                for i in range(0, keys, 128)
            ],
            axis=1,
        )
        values = kvs[:, TW + first : TW + first + 256]
        values = jnp.where(
            (key_column >= used[0]) & (key_column < used[1]), values, jnp.ones_like(values)
        )
        mixed = mm(raised, values)
        if not begins:
            factor = jnp.exp(st_in[rows, :] - best)
            mixed = mixed + jnp.concatenate([factor, factor], axis=1) * acc_in[rows, :]
        if not ends:
            st_out[rows, :] = best
            acc_out[rows, :] = mixed
            continue
        inverse = 1.0 / mixed[:, spare : spare + 1]
        for i, h in enumerate(heads):
            part = slice(i * tokens, (i + 1) * tokens)
            for half in range(2):
                t = first // 128 + half
                a, b = h * TD - t * 128, (h + 1) * TD - t * 128
                if b <= 0 or a >= 128:
                    continue
                keep = (tile_column >= a) & (tile_column < b)
                value = mixed[part, half * 128 : (half + 1) * 128] * inverse[part]
                pieces[t] = jnp.where(keep, value, pieces[t])
    if not ends:
        return
    attended = jnp.concatenate(pieces, axis=1)
    count = info[row]
    atoms = mid.shape[0]
    gated = (attended * sigmoid(query_gate[:, TW:].astype(F32))).astype(BF16)
    fetch.wait()
    final = (hidden_in[...] + mm(gated, proj[...])).astype(BF16)
    token_out[...] = final
    back = mm(final, down[...])
    high = back.astype(BF16)
    rest = back - high.astype(F32)
    low = rest.astype(BF16)
    lowest = (rest - low.astype(F32)).astype(BF16)
    spread = mm(member[...], jnp.concatenate([high, low, lowest], axis=0))
    live = lax.broadcasted_iota(jnp.int32, (atoms, AW), 0) < count
    atom_out[...] = jnp.where(live, mid[...].astype(F32) + spread, 0.0).astype(BF16)


def vmem(count):
    return [pl.BlockSpec(memory_space=VMEM) for _ in range(count)]


def anywhere(count):
    return [pl.BlockSpec(memory_space=pltpu.HBM) for _ in range(count)]


def scalars():
    return [pl.BlockSpec(memory_space=SMEM)]


def like(shape, dtype):
    return jax.ShapeDtypeStruct(shape, dtype)


def solution(mesh):
    width = mesh.shape["row"]
    nchip = width // 2
    groups = [list(range(k, min(k + 4, nchip))) for k in range(0, nchip, 4)]
    if nchip == 8:
        groups = [[0, 1, 2, 4], [3, 5, 6, 7]]

    def swap(value, bits):
        return lax.ppermute(value, "row", [(i, i ^ bits) for i in range(width)])

    def on_device(
        atom_single, atom_count, atom_token, atom_bias, token_single, token_bias, atom_gain,
        atom_qkvg, atom_proj, atom_to_token, token_gain, token_qg, token_kv, token_proj,
        token_to_atom,
    ):
        atoms = atom_single.shape[0]
        tokens = token_single.shape[0]
        rows = LEFT_RIM + atoms + RIGHT_RIM
        far = lax.ppermute(
            atom_single, "row",
            [(i, i + 1 if i % 2 else i - 1) for i in range(1, width - 1)],
        )
        near = swap(atom_single, 1)
        tok = atom_token.reshape(1, atoms)
        gain = atom_gain.reshape(1, AW)
        q, kv, gate, att = pl.pallas_call(
            early_body,
            out_shape=(
                like((atoms, AW), BF16), like((rows, 2 * AW), BF16), like((atoms, AW), BF16),
                like((atoms, AW), F32),
            ),
            in_specs=scalars() + anywhere(2) + vmem(1) + anywhere(1),
            out_specs=tuple(vmem(4)),
            scratch_shapes=[
                VMEM((atoms, AW), BF16), VMEM(atom_bias.shape, BF16), VMEM((AW, 4 * AW), BF16),
                pltpu.SemaphoreType.DMA((4,)),
            ],
            cost_estimate=pl.CostEstimate(
                flops=2 * atoms * AW * (4 * AW + 3 * WK * AH), transcendentals=atoms * AH * WK,
                bytes_accessed=8 << 20,
            ),
            name="early",
        )(atom_count, atom_single, atom_bias, gain, atom_qkvg)
        normed, hidden, mid = pl.pallas_call(
            late_body,
            out_shape=(like((tokens, TW), BF16), like((tokens, TW), F32), like((atoms, AW), BF16)),
            in_specs=scalars() + vmem(9) + anywhere(6),
            out_specs=tuple(vmem(3)),
            scratch_shapes=[
                VMEM((rows, 2 * AW), BF16), VMEM((atoms, AW), F32),
                VMEM((5, AH, WQ, WK), BF16), VMEM((AW, 2 * AW), BF16), VMEM((atoms, AW), BF16),
                VMEM((AW, AW), BF16), VMEM((AW, TW), BF16), VMEM((tokens, TW), BF16),
                pltpu.SemaphoreType.DMA((7,)),
            ],
            compiler_params=pltpu.CompilerParams(vmem_limit_bytes=59200 << 10),
            cost_estimate=pl.CostEstimate(
                flops=4 * atoms * AW * TW, transcendentals=atoms * AH * WK, bytes_accessed=8 << 20,
            ),
            name="late",
        )(
            atom_count, near, far, q, kv, gate, att, tok, gain, token_gain, atom_bias,
            atom_qkvg, atom_single, atom_proj, atom_to_token, token_single,
        )
        blocks, other = {0: normed}, {}
        for k in range(1, nchip):
            top = 1 << (k.bit_length() - 1)
            blocks[k] = swap(normed if k == top else blocks[top], 2 * (k if k == top else k ^ top))
        for k in range(nchip):
            other[k] = swap(blocks[k], 1)
        query_gate, member, normed_again = pl.pallas_call(
            query_body,
            out_shape=(
                like((tokens, 2 * TW), BF16), like((atoms, 3 * tokens), BF16),
                like((tokens, TW), BF16),
            ),
            in_specs=scalars() + vmem(3),
            out_specs=tuple(vmem(3)),
            compiler_params=pltpu.CompilerParams(vmem_limit_bytes=8 << 20),
            name="queries",
        )(atom_count, normed, tok, token_qg)
        blocks[0] = normed_again
        state = ()
        for offsets in groups:
            begin = offsets[0]
            begins, ends = begin == 0, offsets[-1] == nchip - 1
            number = len(offsets)
            keys = number * 2 * tokens
            arrays = [blocks[k] for k in offsets] + [other[k] for k in offsets]
            arrays += [query_gate, token_kv, token_bias, *state]
            specs = vmem(2 * number + 3 + len(state))
            scratch = [
                VMEM((keys, TW), BF16), VMEM((keys, 2 * TW), BF16), VMEM((TH * tokens, 256), BF16),
            ]
            if ends:
                arrays += [atom_count, hidden, mid, member, token_proj, token_to_atom]
                specs += scalars() + vmem(3) + anywhere(1) + vmem(1)
                outs = (like((atoms, AW), BF16), like((tokens, TW), BF16))
                scratch += [VMEM((TW, TW), BF16), pltpu.SemaphoreType.DMA((1,))]
            else:
                outs = (like((TH * tokens, 128), F32), like((TH * tokens, 256), F32))
            state = pl.pallas_call(
                lambda *refs: token_body(offsets, begins, ends, *refs),
                out_shape=outs,
                in_specs=specs,
                out_specs=tuple(vmem(2)),
                scratch_shapes=scratch,
                compiler_params=pltpu.CompilerParams(vmem_limit_bytes=16 << 20),
            )(*arrays)
        return state

    split = P(("sample", "row"), None)
    return jax.shard_map(
        on_device,
        mesh=mesh,
        in_specs=(
            split, P(), P("row"), P("row", None, None, None), split, P(None, "row", None),
            P(), P(), P(), P(), P(), P(), P(), P(), P(),
        ),
        out_specs=(split, split),
        check_vma=False,
    )
```

profile of v0, /device:TPU:0, one launch (start us, length us, event | category | flops | bytes accessed | tf_op | source)
XLA Modules:
  0.0 47.3 jit_solution(14593696963393203747)
XLA Ops:
  0.6 0.0 copy-start.9
  0.6 0.0 copy-start.8
  0.7 0.6 %collective-permute-start = (bf16[512,128]{1,0:T(8,128)(2,1)}, bf16[512,128]{1,0:T(8,128)(2,1)S(1)}, u32[]{:S(2)}, u32[]{:S(2)}) collective-permute-start(bf16[512,128]{1,0:T(8,128)(2,1)} %x_hbm.3), channel_id=1, source_target_pairs={{0,1},{1,0},{2,3},{3,2},{4,5},{5,4},{6,7},{7,6},{8,9},{9,8},{10,11... | collective-permute-start | bytes 393224 | tf_op jit(solution)/shard_map/ppermute | solution.py:344
  1.2 0.7 %collective-permute-start.1 = (bf16[512,128]{1,0:T(8,128)(2,1)}, bf16[512,128]{1,0:T(8,128)(2,1)S(1)}, u32[]{:S(2)}, u32[]{:S(2)}) collective-permute-start(bf16[512,128]{1,0:T(8,128)(2,1)} %x_hbm.3), channel_id=1, source_target_pairs={{1,2},{2,1},{3,4},{4,3},{5,6},{6,5},{7,8},{8,7},{9,10},{10,9},{11,... | collective-permute-start | bytes 393224 | tf_op jit(solution)/shard_map/ppermute | solution.py:354
  1.9 4.1 %early.1 = (bf16[512,128]{1,0:T(8,128)(2,1)}, bf16[640,256]{1,0:T(8,128)(2,1)}, bf16[512,128]{1,0:T(8,128)(2,1)}, f32[512,128]{1,0:T(8,128)}) custom-call(s32[16]{0:T(128)} %refs_13_.1, bf16[512,128]{1,0:T(8,128)(2,1)} %x_hbm.3, bf16[16,4,32,128]{3,2,1,0:T(8,128)(2,1)} %bias.1, f32[1,128]{1,0:T(1,128)} %bitcast.4, bf16[128,512]{1,0:T(8,128)(2,1)} %qkvg_hbm.3), custom_call_target="tpu_custom_call" | custom-call | flops 268435456 | bytes 8388608 | tf_op jit(solution)/shard_map/early/pallas_call | solution.py:361
  6.0 0.0 copy-start
  6.0 0.0 copy-start.1
  6.0 0.0 collective-permute-done.near
  6.1 0.0 copy-start.10
  6.1 0.0 collective-permute-done.1.far
  6.1 0.0 copy-start.11
  6.1 0.6 %copy-done.10 = bf16[512,128]{1,0:T(8,128)(2,1)} copy-done((bf16[512,128]{1,0:T(8,128)(2,1)}, bf16[512,128]{1,0:T(8,128)(2,1)S(1)}, u32[]{:S(2)}) %copy-start.10) | copy-done | bytes 131096
  6.7 0.0 copy-done.11
  6.8 5.2 %late.1 = (bf16[64,768]{1,0:T(8,128)(2,1)}, f32[64,768]{1,0:T(8,128)}, bf16[512,128]{1,0:T(8,128)(2,1)}) custom-call(s32[16]{0:T(128)} %refs_13_.1, bf16[512,128]{1,0:T(8,128)(2,1)} %copy-done.10, bf16[512,128]{1,0:T(8,128)(2,1)} %copy-done.11, bf16[512,128]{1,0:T(8,128)(2,1)} %get-tuple-element.14.q, bf16[640,256]{1,0:T(8,128)(2,1)} %get-tuple-element.15.kv_in, ...), custom_call_target="tpu_custom_call" | custom-call | flops 201326592 | bytes 8388608 | tf_op jit(solution)/shard_map/late/pallas_call | solution.py:379
  12.0 6.4 %collective-permute-start.4 = (bf16[64,768]{1,0:T(8,128)(2,1)}, bf16[64,768]{1,0:T(8,128)(2,1)S(1)}, u32[]{:S(2)}, u32[]{:S(2)}) collective-permute-start(bf16[64,768]{1,0:T(8,128)(2,1)} %get-tuple-element.18.normed), channel_id=1, source_target_pairs={{0,8},{1,9},{2,10},{3,11},{4,12},{5,13},{6,14},{7,15},{8,0},{9,1},... | collective-permute-start | bytes 294920 | tf_op jit(solution)/shard_map/ppermute | solution.py:344
  18.4 1.6 %collective-permute-start.2 = (bf16[64,768]{1,0:T(8,128)(2,1)}, bf16[64,768]{1,0:T(8,128)(2,1)S(1)}, u32[]{:S(2)}, u32[]{:S(2)}) collective-permute-start(bf16[64,768]{1,0:T(8,128)(2,1)} %get-tuple-element.18.normed), channel_id=1, source_target_pairs={{0,4},{1,5},{2,6},{3,7},{4,0},{5,1},{6,2},{7,3},{8,12},{9,13},{10,... | collective-permute-start | bytes 294920 | tf_op jit(solution)/shard_map/ppermute | solution.py:344
  20.0 0.6 %collective-permute-start.12 = (bf16[64,768]{1,0:T(8,128)(2,1)}, bf16[64,768]{1,0:T(8,128)(2,1)S(1)}, u32[]{:S(2)}, u32[]{:S(2)}) collective-permute-start(bf16[64,768]{1,0:T(8,128)(2,1)} %get-tuple-element.18.normed), channel_id=1, source_target_pairs={{0,2},{1,3},{2,0},{3,1},{4,6},{5,7},{6,4},{7,5},{8,10},{9,11},{10,... | collective-permute-start | bytes 294920 | tf_op jit(solution)/shard_map/ppermute | solution.py:344
  20.6 0.0 collective-permute-start.13
  20.6 3.6 %collective-permute-done.4.refs_3_ = bf16[64,768]{1,0:T(8,128)(2,1)S(1)} collective-permute-done((bf16[64,768]{1,0:T(8,128)(2,1)}, bf16[64,768]{1,0:T(8,128)(2,1)S(1)}, u32[]{:S(2)}, u32[]{:S(2)}) %collective-permute-start.4) | collective-permute-done | bytes 98336 | tf_op jit(solution)/shard_map/ppermute | solution.py:344
  24.2 0.0 collective-permute-start.16
  24.2 0.2 collective-permute-done.2.refs_2_
  24.4 0.3 collective-permute-start.15
  24.7 1.1 %collective-permute-start.6 = (bf16[64,768]{1,0:T(8,128)(2,1)S(1)}, bf16[64,768]{1,0:T(8,128)(2,1)S(1)}, u32[]{:S(2)}, u32[]{:S(2)}) collective-permute-start(bf16[64,768]{1,0:T(8,128)(2,1)S(1)} %collective-permute-done.4.refs_3_), channel_id=1, source_target_pairs={{0,4},{1,5},{2,6},{3,7},{4,0},{5,1},{6,2},{7,3},{8,12},{9,13},{10,... | collective-permute-start | bytes 294920 | tf_op jit(solution)/shard_map/ppermute | solution.py:344
  25.8 0.0 collective-permute-done.12.refs_1_
  25.8 1.2 %collective-permute-start.7 = (bf16[64,768]{1,0:T(8,128)(2,1)S(1)}, bf16[64,768]{1,0:T(8,128)(2,1)S(1)}, u32[]{:S(2)}, u32[]{:S(2)}) collective-permute-start(bf16[64,768]{1,0:T(8,128)(2,1)S(1)} %collective-permute-done.4.refs_3_), channel_id=1, source_target_pairs={{0,6},{1,7},{2,4},{3,5},{4,2},{5,3},{6,0},{7,1},{8,14},{9,15},{10,... | collective-permute-start | bytes 294920 | tf_op jit(solution)/shard_map/ppermute | solution.py:344
  27.1 0.0 collective-permute-done.13.refs_4_
  27.1 1.1 %collective-permute-start.5 = (bf16[64,768]{1,0:T(8,128)(2,1)S(1)}, bf16[64,768]{1,0:T(8,128)(2,1)S(1)}, u32[]{:S(2)}, u32[]{:S(2)}) collective-permute-start(bf16[64,768]{1,0:T(8,128)(2,1)S(1)} %collective-permute-done.4.refs_3_), channel_id=1, source_target_pairs={{0,2},{1,3},{2,0},{3,1},{4,6},{5,7},{6,4},{7,5},{8,10},{9,11},{10,... | collective-permute-start | bytes 294920 | tf_op jit(solution)/shard_map/ppermute | solution.py:344
  28.2 0.0 collective-permute-done.16.refs_7_
  28.2 0.9 %collective-permute-start.3 = (bf16[64,768]{1,0:T(8,128)(2,1)S(1)}, bf16[64,768]{1,0:T(8,128)(2,1)S(1)}, u32[]{:S(2)}, u32[]{:S(2)}) collective-permute-start(bf16[64,768]{1,0:T(8,128)(2,1)S(1)} %collective-permute-done.2.refs_2_), channel_id=1, source_target_pairs={{0,2},{1,3},{2,0},{3,1},{4,6},{5,7},{6,4},{7,5},{8,10},{9,11},{10,... | collective-permute-start | bytes 294920 | tf_op jit(solution)/shard_map/ppermute | solution.py:344
  29.1 0.0 collective-permute-done.15.refs_6_
  29.1 0.0 collective-permute-start.14
  29.1 1.0 %collective-permute-done.6.refs_2_ = bf16[64,768]{1,0:T(8,128)(2,1)S(1)} collective-permute-done((bf16[64,768]{1,0:T(8,128)(2,1)S(1)}, bf16[64,768]{1,0:T(8,128)(2,1)S(1)}, u32[]{:S(2)}, u32[]{:S(2)}) %collective-permute-start.6) | collective-permute-done | bytes 98336 | tf_op jit(solution)/shard_map/ppermute | solution.py:344
  30.1 0.0 collective-permute-start.10
  30.1 2.3 %collective-permute-done.7.refs_3_ = bf16[64,768]{1,0:T(8,128)(2,1)S(1)} collective-permute-done((bf16[64,768]{1,0:T(8,128)(2,1)S(1)}, bf16[64,768]{1,0:T(8,128)(2,1)S(1)}, u32[]{:S(2)}, u32[]{:S(2)}) %collective-permute-start.7) | collective-permute-done | bytes 98336 | tf_op jit(solution)/shard_map/ppermute | solution.py:344
  32.4 0.0 collective-permute-start.11
  32.4 2.0 %collective-permute-done.5.refs_1_ = bf16[64,768]{1,0:T(8,128)(2,1)S(1)} collective-permute-done((bf16[64,768]{1,0:T(8,128)(2,1)S(1)}, bf16[64,768]{1,0:T(8,128)(2,1)S(1)}, u32[]{:S(2)}, u32[]{:S(2)}) %collective-permute-start.5) | collective-permute-done | bytes 98336 | tf_op jit(solution)/shard_map/ppermute | solution.py:344
  34.4 0.0 collective-permute-start.9
  34.4 1.5 %collective-permute-done.3.refs_0_ = bf16[64,768]{1,0:T(8,128)(2,1)S(1)} collective-permute-done((bf16[64,768]{1,0:T(8,128)(2,1)S(1)}, bf16[64,768]{1,0:T(8,128)(2,1)S(1)}, u32[]{:S(2)}, u32[]{:S(2)}) %collective-permute-start.3) | collective-permute-done | bytes 98336 | tf_op jit(solution)/shard_map/ppermute | solution.py:344
  35.9 0.0 collective-permute-start.8
  35.9 0.0 copy-done.9
  35.9 0.0 copy-done.8
  35.9 0.0 copy-start.2
  35.9 1.7 %copy-done.2 = bf16[768,1536]{1,0:T(8,128)(2,1)S(1)} copy-done((bf16[768,1536]{1,0:T(8,128)(2,1)S(1)}, bf16[768,1536]{1,0:T(8,128)(2,1)}, u32[]{:S(2)}) %copy-start.2) | copy-done | bytes 2359320
  37.6 0.0 copy-start.7
  37.6 0.9 %copy-done.7 = bf16[64,768]{1,0:T(8,128)(2,1)S(1)} copy-done((bf16[64,768]{1,0:T(8,128)(2,1)S(1)}, bf16[64,768]{1,0:T(8,128)(2,1)}, u32[]{:S(2)}) %copy-start.7) | copy-done | bytes 98328
  38.5 1.2 %queries.1 = (bf16[64,1536]{1,0:T(8,128)(2,1)S(1)}, bf16[512,192]{1,0:T(8,128)(2,1)S(1)}, bf16[64,768]{1,0:T(8,128)(2,1)S(1)}) custom-call(s32[16]{0:T(128)S(1)} %copy-done.9, bf16[64,768]{1,0:T(8,128)(2,1)S(1)} %copy-done.7, s32[1,512]{1,0:T(1,128)S(1)} %bitcast.3, bf16[768,1536]{1,0:T(8,128)(2,1)S(1)} %copy-done.2), custom_call_target="tpu_custom_call" | custom-call | tf_op jit(solution)/shard_map/queries/pallas_call | solution.py:405
  39.6 0.0 collective-permute-done.14.refs_5_
  39.6 0.0 copy-done
  39.7 0.0 copy-done.1
  39.7 0.0 copy-start.3
  39.7 0.0 copy-start.4
  39.7 0.0 copy-start.5
  39.7 0.0 copy-start.6
  39.7 2.5 %shard_map.158 = (f32[1024,128]{1,0:T(8,128)S(1)}, f32[1024,256]{1,0:T(8,128)S(1)}) custom-call(bf16[64,768]{1,0:T(8,128)(2,1)S(1)} %get-tuple-element.20.refs_0_, bf16[64,768]{1,0:T(8,128)(2,1)S(1)} %collective-permute-done.12.refs_1_, bf16[64,768]{1,0:T(8,128)(2,1)S(1)} %collective-permute-done.2.refs_2_, ...), custom_call_target="tpu_custom_call" | custom-call | tf_op jit(solution)/shard_map/pallas_call | solution.py:436
  42.2 0.0 collective-permute-done.10.refs_6_
  42.3 0.0 collective-permute-done.11.refs_7_
  42.3 0.0 collective-permute-done.9.refs_5_
  42.3 0.0 collective-permute-done.8.refs_4_
  42.3 0.0 copy-done.3
  42.3 0.0 copy-done.4
  42.3 0.0 copy-done.5
  42.3 0.0 copy-done.6
  42.3 5.0 %shard_map.159 = (bf16[512,128]{1,0:T(8,128)(2,1)}, bf16[64,768]{1,0:T(8,128)(2,1)}) custom-call(bf16[64,768]{1,0:T(8,128)(2,1)S(1)} %collective-permute-done.3.refs_0_, bf16[64,768]{1,0:T(8,128)(2,1)S(1)} %collective-permute-done.5.refs_1_, bf16[64,768]{1,0:T(8,128)(2,1)S(1)} %collective-permute-done.6.refs_2_, ...), custom_call_target="tpu_custom_call" | custom-call | tf_op jit(solution)/shard_map/pallas_call | solution.py:436
Async XLA Ops:
  0.6 35.3 %copy-start.9 = (s32[16]{0:T(128)S(1)}, s32[16]{0:T(128)}, u32[]{:S(2)}) copy-start(s32[16]{0:T(128)} %refs_13_.1) | copy-start | bytes 196
  0.6 35.2 %copy-start.8 = (s32[512]{0:T(512)S(1)}, s32[512]{0:T(512)}, u32[]{:S(2)}) copy-start(s32[512]{0:T(512)} %param.17) | copy-start | bytes 6148
  0.7 5.4 %collective-permute-start = (bf16[512,128]{1,0:T(8,128)(2,1)}, bf16[512,128]{1,0:T(8,128)(2,1)S(1)}, u32[]{:S(2)}, u32[]{:S(2)}) collective-permute-start(bf16[512,128]{1,0:T(8,128)(2,1)} %x_hbm.3), channel_id=1, source_target_pairs={{0,1},{1,0},{2,3},{3,2},{4,5},{5,4},{6,7},{7,6},{8,9},{9,8},{10,11... | collective-permute-start | bytes 393224 | tf_op jit(solution)/shard_map/ppermute | solution.py:344
  1.2 4.9 %collective-permute-start.1 = (bf16[512,128]{1,0:T(8,128)(2,1)}, bf16[512,128]{1,0:T(8,128)(2,1)S(1)}, u32[]{:S(2)}, u32[]{:S(2)}) collective-permute-start(bf16[512,128]{1,0:T(8,128)(2,1)} %x_hbm.3), channel_id=1, source_target_pairs={{1,2},{2,1},{3,4},{4,3},{5,6},{6,5},{7,8},{8,7},{9,10},{10,9},{11,... | collective-permute-start | bytes 393224 | tf_op jit(solution)/shard_map/ppermute | solution.py:354
  6.0 33.6 %copy-start = (bf16[768,1536]{1,0:T(8,128)(2,1)S(1)}, bf16[768,1536]{1,0:T(8,128)(2,1)}, u32[]{:S(2)}) copy-start(bf16[768,1536]{1,0:T(8,128)(2,1)} %refs_9_.3) | copy-start | bytes 7077892
  6.0 33.6 %copy-start.1 = (bf16[16,64,1024]{2,1,0:T(8,128)(2,1)S(1)}, bf16[16,64,1024]{2,1,0:T(8,128)(2,1)}, u32[]{:S(2)}) copy-start(bf16[16,64,1024]{2,1,0:T(8,128)(2,1)} %refs_10_.3) | copy-start | bytes 6291460
  6.1 0.7 %copy-start.10 = (bf16[512,128]{1,0:T(8,128)(2,1)}, bf16[512,128]{1,0:T(8,128)(2,1)S(1)}, u32[]{:S(2)}) copy-start(bf16[512,128]{1,0:T(8,128)(2,1)S(1)} %collective-permute-done.near) | copy-start | bytes 393220
  6.1 0.7 %copy-start.11 = (bf16[512,128]{1,0:T(8,128)(2,1)}, bf16[512,128]{1,0:T(8,128)(2,1)S(1)}, u32[]{:S(2)}) copy-start(bf16[512,128]{1,0:T(8,128)(2,1)S(1)} %collective-permute-done.1.far) | copy-start | bytes 393220
  12.0 12.2 %collective-permute-start.4 = (bf16[64,768]{1,0:T(8,128)(2,1)}, bf16[64,768]{1,0:T(8,128)(2,1)S(1)}, u32[]{:S(2)}, u32[]{:S(2)}) collective-permute-start(bf16[64,768]{1,0:T(8,128)(2,1)} %get-tuple-element.18.normed), channel_id=1, source_target_pairs={{0,8},{1,9},{2,10},{3,11},{4,12},{5,13},{6,14},{7,15},{8,0},{9,1},... | collective-permute-start | bytes 294920 | tf_op jit(solution)/shard_map/ppermute | solution.py:344
  18.4 6.0 %collective-permute-start.2 = (bf16[64,768]{1,0:T(8,128)(2,1)}, bf16[64,768]{1,0:T(8,128)(2,1)S(1)}, u32[]{:S(2)}, u32[]{:S(2)}) collective-permute-start(bf16[64,768]{1,0:T(8,128)(2,1)} %get-tuple-element.18.normed), channel_id=1, source_target_pairs={{0,4},{1,5},{2,6},{3,7},{4,0},{5,1},{6,2},{7,3},{8,12},{9,13},{10,... | collective-permute-start | bytes 294920 | tf_op jit(solution)/shard_map/ppermute | solution.py:344
  20.0 5.9 %collective-permute-start.12 = (bf16[64,768]{1,0:T(8,128)(2,1)}, bf16[64,768]{1,0:T(8,128)(2,1)S(1)}, u32[]{:S(2)}, u32[]{:S(2)}) collective-permute-start(bf16[64,768]{1,0:T(8,128)(2,1)} %get-tuple-element.18.normed), channel_id=1, source_target_pairs={{0,2},{1,3},{2,0},{3,1},{4,6},{5,7},{6,4},{7,5},{8,10},{9,11},{10,... | collective-permute-start | bytes 294920 | tf_op jit(solution)/shard_map/ppermute | solution.py:344
  20.6 6.5 %collective-permute-start.13 = (bf16[64,768]{1,0:T(8,128)(2,1)}, bf16[64,768]{1,0:T(8,128)(2,1)S(1)}, u32[]{:S(2)}, u32[]{:S(2)}) collective-permute-start(bf16[64,768]{1,0:T(8,128)(2,1)} %get-tuple-element.18.normed), channel_id=1, source_target_pairs={{0,1},{1,0},{2,3},{3,2},{4,5},{5,4},{6,7},{7,6},{8,9},{9,8},{10,11... | collective-permute-start | bytes 294920 | tf_op jit(solution)/shard_map/ppermute | solution.py:344
  24.2 4.0 %collective-permute-start.16 = (bf16[64,768]{1,0:T(8,128)(2,1)S(1)}, bf16[64,768]{1,0:T(8,128)(2,1)S(1)}, u32[]{:S(2)}, u32[]{:S(2)}) collective-permute-start(bf16[64,768]{1,0:T(8,128)(2,1)S(1)} %collective-permute-done.4.refs_3_), channel_id=1, source_target_pairs={{0,1},{1,0},{2,3},{3,2},{4,5},{5,4},{6,7},{7,6},{8,9},{9,8},{10,11... | collective-permute-start | bytes 294920 | tf_op jit(solution)/shard_map/ppermute | solution.py:344
  24.4 4.7 %collective-permute-start.15 = (bf16[64,768]{1,0:T(8,128)(2,1)S(1)}, bf16[64,768]{1,0:T(8,128)(2,1)S(1)}, u32[]{:S(2)}, u32[]{:S(2)}) collective-permute-start(bf16[64,768]{1,0:T(8,128)(2,1)S(1)} %collective-permute-done.2.refs_2_), channel_id=1, source_target_pairs={{0,1},{1,0},{2,3},{3,2},{4,5},{5,4},{6,7},{7,6},{8,9},{9,8},{10,11... | collective-permute-start | bytes 294920 | tf_op jit(solution)/shard_map/ppermute | solution.py:344
  24.7 5.4 %collective-permute-start.6 = (bf16[64,768]{1,0:T(8,128)(2,1)S(1)}, bf16[64,768]{1,0:T(8,128)(2,1)S(1)}, u32[]{:S(2)}, u32[]{:S(2)}) collective-permute-start(bf16[64,768]{1,0:T(8,128)(2,1)S(1)} %collective-permute-done.4.refs_3_), channel_id=1, source_target_pairs={{0,4},{1,5},{2,6},{3,7},{4,0},{5,1},{6,2},{7,3},{8,12},{9,13},{10,... | collective-permute-start | bytes 294920 | tf_op jit(solution)/shard_map/ppermute | solution.py:344
  25.8 6.6 %collective-permute-start.7 = (bf16[64,768]{1,0:T(8,128)(2,1)S(1)}, bf16[64,768]{1,0:T(8,128)(2,1)S(1)}, u32[]{:S(2)}, u32[]{:S(2)}) collective-permute-start(bf16[64,768]{1,0:T(8,128)(2,1)S(1)} %collective-permute-done.4.refs_3_), channel_id=1, source_target_pairs={{0,6},{1,7},{2,4},{3,5},{4,2},{5,3},{6,0},{7,1},{8,14},{9,15},{10,... | collective-permute-start | bytes 294920 | tf_op jit(solution)/shard_map/ppermute | solution.py:344
  27.1 7.3 %collective-permute-start.5 = (bf16[64,768]{1,0:T(8,128)(2,1)S(1)}, bf16[64,768]{1,0:T(8,128)(2,1)S(1)}, u32[]{:S(2)}, u32[]{:S(2)}) collective-permute-start(bf16[64,768]{1,0:T(8,128)(2,1)S(1)} %collective-permute-done.4.refs_3_), channel_id=1, source_target_pairs={{0,2},{1,3},{2,0},{3,1},{4,6},{5,7},{6,4},{7,5},{8,10},{9,11},{10,... | collective-permute-start | bytes 294920 | tf_op jit(solution)/shard_map/ppermute | solution.py:344
  28.2 7.7 %collective-permute-start.3 = (bf16[64,768]{1,0:T(8,128)(2,1)S(1)}, bf16[64,768]{1,0:T(8,128)(2,1)S(1)}, u32[]{:S(2)}, u32[]{:S(2)}) collective-permute-start(bf16[64,768]{1,0:T(8,128)(2,1)S(1)} %collective-permute-done.2.refs_2_), channel_id=1, source_target_pairs={{0,2},{1,3},{2,0},{3,1},{4,6},{5,7},{6,4},{7,5},{8,10},{9,11},{10,... | collective-permute-start | bytes 294920 | tf_op jit(solution)/shard_map/ppermute | solution.py:344
  29.1 10.5 %collective-permute-start.14 = (bf16[64,768]{1,0:T(8,128)(2,1)S(1)}, bf16[64,768]{1,0:T(8,128)(2,1)S(1)}, u32[]{:S(2)}, u32[]{:S(2)}) collective-permute-start(bf16[64,768]{1,0:T(8,128)(2,1)S(1)} %collective-permute-done.12.refs_1_), channel_id=1, source_target_pairs={{0,1},{1,0},{2,3},{3,2},{4,5},{5,4},{6,7},{7,6},{8,9},{9,8},{10,11... | collective-permute-start | bytes 294920 | tf_op jit(solution)/shard_map/ppermute | solution.py:344
  30.1 12.1 %collective-permute-start.10 = (bf16[64,768]{1,0:T(8,128)(2,1)S(1)}, bf16[64,768]{1,0:T(8,128)(2,1)S(1)}, u32[]{:S(2)}, u32[]{:S(2)}) collective-permute-start(bf16[64,768]{1,0:T(8,128)(2,1)S(1)} %collective-permute-done.6.refs_2_), channel_id=1, source_target_pairs={{0,1},{1,0},{2,3},{3,2},{4,5},{5,4},{6,7},{7,6},{8,9},{9,8},{10,11... | collective-permute-start | bytes 294920 | tf_op jit(solution)/shard_map/ppermute | solution.py:344
  32.4 9.9 %collective-permute-start.11 = (bf16[64,768]{1,0:T(8,128)(2,1)S(1)}, bf16[64,768]{1,0:T(8,128)(2,1)S(1)}, u32[]{:S(2)}, u32[]{:S(2)}) collective-permute-start(bf16[64,768]{1,0:T(8,128)(2,1)S(1)} %collective-permute-done.7.refs_3_), channel_id=1, source_target_pairs={{0,1},{1,0},{2,3},{3,2},{4,5},{5,4},{6,7},{7,6},{8,9},{9,8},{10,11... | collective-permute-start | bytes 294920 | tf_op jit(solution)/shard_map/ppermute | solution.py:344
  34.4 7.9 %collective-permute-start.9 = (bf16[64,768]{1,0:T(8,128)(2,1)S(1)}, bf16[64,768]{1,0:T(8,128)(2,1)S(1)}, u32[]{:S(2)}, u32[]{:S(2)}) collective-permute-start(bf16[64,768]{1,0:T(8,128)(2,1)S(1)} %collective-permute-done.5.refs_1_), channel_id=1, source_target_pairs={{0,1},{1,0},{2,3},{3,2},{4,5},{5,4},{6,7},{7,6},{8,9},{9,8},{10,11... | collective-permute-start | bytes 294920 | tf_op jit(solution)/shard_map/ppermute | solution.py:344
  35.9 6.4 %collective-permute-start.8 = (bf16[64,768]{1,0:T(8,128)(2,1)S(1)}, bf16[64,768]{1,0:T(8,128)(2,1)S(1)}, u32[]{:S(2)}, u32[]{:S(2)}) collective-permute-start(bf16[64,768]{1,0:T(8,128)(2,1)S(1)} %collective-permute-done.3.refs_0_), channel_id=1, source_target_pairs={{0,1},{1,0},{2,3},{3,2},{4,5},{5,4},{6,7},{7,6},{8,9},{9,8},{10,11... | collective-permute-start | bytes 294920 | tf_op jit(solution)/shard_map/ppermute | solution.py:344
  35.9 1.7 %copy-start.2 = (bf16[768,1536]{1,0:T(8,128)(2,1)S(1)}, bf16[768,1536]{1,0:T(8,128)(2,1)}, u32[]{:S(2)}) copy-start(bf16[768,1536]{1,0:T(8,128)(2,1)} %qg.1) | copy-start | bytes 7077892
  37.6 0.9 %copy-start.7 = (bf16[64,768]{1,0:T(8,128)(2,1)S(1)}, bf16[64,768]{1,0:T(8,128)(2,1)}, u32[]{:S(2)}) copy-start(bf16[64,768]{1,0:T(8,128)(2,1)} %get-tuple-element.18.normed) | copy-start | bytes 294916
  39.7 2.6 %copy-start.3 = (bf16[768,768]{1,0:T(8,128)(2,1)S(1)}, bf16[768,768]{1,0:T(8,128)(2,1)}, u32[]{:S(2)}) copy-start(bf16[768,768]{1,0:T(8,128)(2,1)} %refs_17_.1) | copy-start | bytes 3538948
  39.7 2.6 %copy-start.4 = (bf16[768,128]{1,0:T(8,128)(2,1)S(1)}, bf16[768,128]{1,0:T(8,128)(2,1)}, u32[]{:S(2)}) copy-start(bf16[768,128]{1,0:T(8,128)(2,1)} %refs_18_.1) | copy-start | bytes 589828
  39.7 2.6 %copy-start.5 = (f32[64,768]{1,0:T(8,128)S(1)}, f32[64,768]{1,0:T(8,128)}, u32[]{:S(2)}) copy-start(f32[64,768]{1,0:T(8,128)} %get-tuple-element.23.refs_14_) | copy-start | bytes 589828
  39.7 2.6 %copy-start.6 = (bf16[512,128]{1,0:T(8,128)(2,1)S(1)}, bf16[512,128]{1,0:T(8,128)(2,1)}, u32[]{:S(2)}) copy-start(bf16[512,128]{1,0:T(8,128)(2,1)} %get-tuple-element.24.refs_15_) | copy-start | bytes 393220
where the time goes:
time: 47.6 us; the launch traced here: 47.3 us
  Pallas kernels  18.1 us (38%)
  starting transfers between devices  14.5 us (30%)
  waiting for transfers between devices  10.5 us (22%)
  local copies, waits for them, and re-layouts  3.28 us (7%)
  between operations  0.86 us (2%)
    ppermute x16, starting transfers between devices, swap(): return lax.ppermute(value, 'row', [(i, i ^ bits) for i in range(width)])  13.9 us
    ppermute x16, waiting for transfers between devices, swap(): return lax.ppermute(value, 'row', [(i, i ^ bits) for i in range(width)])  10.5 us
    pallas_call x2, Pallas kernels, on_device(): pl.pallas_call(lambda *refs: token_body(offsets, begins, ends, *refs), ou...  7.53 us
    pallas_call x1, Pallas kernels, on_device(): pl.pallas_call(late_body, out_shape=(like((tokens, TW), BF16), like((toke...  5.25 us
    pallas_call x1, Pallas kernels, on_device(): pl.pallas_call(early_body, out_shape=(like((atoms, AW), BF16), like((rows...  4.14 us
    unnamed x24, local copies, waits for them, and re-layouts  3.28 us
    pallas_call x1, Pallas kernels, on_device(): pl.pallas_call(query_body, out_shape=(like((tokens, 2 * TW), BF16), like(...  1.18 us
  transfers between devices with their start and end apart: 17, of which 6 were waited for; matrix products, arithmetic and copies ran while one was open for 0% of the time, Pallas kernels for 17%

commit v1 on v0

--- a/solution.py
+++ b/solution.py
@@ -73,24 +73,11 @@
     return out
 
 
-def early_body(
-    info, x_hbm, bias_hbm, gain, qkvg_hbm, q_out, kv_out, gate_out, att_out, x, bias, qkvg, sems
-):
+def early_body(info, x, bias, gain, qkvg, q_out, kv_out, gate_out, gated_out):
     row = lax.axis_index("row")
     count = info[row]
     atoms = x.shape[0]
-    half = atoms // WQ // 2
-    copies = [
-        pltpu.make_async_copy(x_hbm, x, sems.at[0]),
-        pltpu.make_async_copy(qkvg_hbm, qkvg, sems.at[1]),
-        pltpu.make_async_copy(bias_hbm.at[:half], bias.at[:half], sems.at[2]),
-        pltpu.make_async_copy(bias_hbm.at[half:], bias.at[half:], sems.at[3]),
-    ]
-    for copy in copies:
-        copy.start()
-    copies[0].wait()
     normed = normalise(x[...].astype(F32), gain[...])
-    copies[1].wait()
     parts = mm(normed, qkvg[...]).astype(BF16)
     q_out[...] = parts[:, :AW]
     gate_out[...] = parts[:, 3 * AW :]
@@ -98,19 +85,18 @@
     kv_out[LEFT_RIM : LEFT_RIM + atoms, :] = parts[:, AW : 3 * AW]
     kv_out[LEFT_RIM + atoms :, :] = jnp.zeros((RIGHT_RIM, 2 * AW), BF16)
     for w in range(atoms // WQ):
-        if w % half == 0:
-            copies[2 + w // half].wait()
         rows = slice(WQ * w, WQ * w + WK)
-        att_out[WQ * w : WQ * (w + 1), :] = attend_window(
-            q_out[WQ * w : WQ * (w + 1), :], kv_out[rows, :AW], kv_out[rows, AW:],
+        own = slice(WQ * w, WQ * (w + 1))
+        out = attend_window(
+            q_out[own, :], kv_out[rows, :AW], kv_out[rows, AW:],
             bias[w], WQ * w - LEFT_RIM, 0, count,
         )
+        gated_out[own, :] = (out * sigmoid(gate_out[own, :].astype(F32))).astype(BF16)
 
 
 def late_body(
-    info, near, far, q, kv_in, gate_in, att_in, tok, gain, tgain, bias, qkvg_hbm, x_hbm, proj_hbm,
-    lift_hbm, tsingle_hbm, normed_out, hidden_out, mid_out, kv, att, some, qkvg, x, proj, lift,
-    tsingle, sems,
+    info, near, far, q, kv_in, gate_in, gated_in, tok, gain, tgain, bias, qkvg, x, proj, lift,
+    tsingle, normed_out, hidden_out, mid_out, kv, gated,
 ):
     row = lax.axis_index("row")
     width = lax.axis_size("row")
@@ -118,21 +104,6 @@
     atoms = x.shape[0]
     tokens = tsingle.shape[0]
     last = (count - 1) // WQ
-    head = pltpu.make_async_copy(bias.at[0:2], some.at[0:2], sems.at[0])
-    head.start()
-    tail = pltpu.make_async_copy(bias.at[pl.ds(last - 2, 3)], some.at[2:5], sems.at[1])
-    tail.start()
-    copies = [
-        pltpu.make_async_copy(source, target, sems.at[2 + i])
-        for i, (source, target) in enumerate(
-            [
-                (qkvg_hbm.at[:, AW : 3 * AW], qkvg), (x_hbm, x), (proj_hbm, proj),
-                (lift_hbm, lift), (tsingle_hbm, tsingle),
-            ]
-        )
-    ]
-    for copy in copies:
-        copy.start()
     odd = row % 2 == 1
     previous = jnp.where(odd, near[...], far[...])
     following = jnp.where(odd, far[0:RIGHT_RIM, :], near[0:RIGHT_RIM, :])
@@ -141,13 +112,11 @@
     pick = r == lax.broadcasted_iota(jnp.int32, (LEFT_RIM, atoms), 1)
     before = mm(jnp.where(pick, 1.0, 0.0).astype(BF16), previous)
     rims = jnp.concatenate([before, following.astype(F32)], axis=0)
-    rims = normalise(rims, gain[...])
-    copies[0].wait()
-    rim_kv = mm(rims, qkvg[...]).astype(BF16)
+    rim_kv = mm(normalise(rims, gain[...]), qkvg[:, AW : 3 * AW]).astype(BF16)
     after_kv = rim_kv[LEFT_RIM:]
     kv[...] = kv_in[...]
     kv[0:LEFT_RIM, :] = rim_kv[:LEFT_RIM]
-    att[...] = att_in[...]
+    gated[...] = gated_in[...]
     low = jnp.where(row == 0, 0, -4 * atoms)
     high = jnp.where(row == width - 1, count, 4 * atoms)
     region = 2 * WQ + WK
@@ -158,32 +127,25 @@
     r = lax.broadcasted_iota(jnp.int32, (region, 2 * AW), 0) + (start - LEFT_RIM - count)
     local = kv[pl.ds(start, region), :].astype(F32)
     local = jnp.where((r >= 0) & (r < RIGHT_RIM), moved, local).astype(BF16)
-    head.wait()
-    tail.wait()
-    for w in range(2):
-        rows = slice(WQ * w, WQ * w + WK)
-        att[WQ * w : WQ * (w + 1), :] = attend_window(
-            q[WQ * w : WQ * (w + 1), :], kv[rows, :AW], kv[rows, AW:], some[w],
-            WQ * w - LEFT_RIM, low, high,
-        )
-    for w in range(3):
-        at = pl.multiple_of(start + WQ * w, WQ)
-        rows = slice(WQ * w, WQ * w + WK)
-        att[pl.ds(at, WQ), :] = attend_window(
-            q[pl.ds(at, WQ), :], local[rows, :AW], local[rows, AW:], some[2 + w],
-            at - LEFT_RIM, low, high,
-        )
-    gated = (att[...] * sigmoid(gate_in[...].astype(F32))).astype(BF16)
-    copies[1].wait()
-    copies[2].wait()
-    mid = (x[...].astype(F32) + mm(gated, proj[...])).astype(BF16)
-    mid_out[...] = mid
-    copies[3].wait()
+    for w in range(5):
+        if w < 2:
+            at, base, source, bias_at = WQ * w, WQ * w, kv, w
+        else:
+            at = pl.multiple_of(start + WQ * (w - 2), WQ)
+            base, source, bias_at = WQ * (w - 2), local, last + (w - 4)
+        rows, own = slice(base, base + WK), pl.ds(at, WQ)
+        out = attend_window(
+            q[own, :], source[rows, :AW], source[rows, AW:], bias[bias_at], at - LEFT_RIM, low,
+            high,
+        )
+        gated[own, :] = (out * sigmoid(gate_in[own, :].astype(F32))).astype(BF16)
+    mid = (x[...].astype(F32) + mm(gated[...], proj[...])).astype(BF16)
+    live = lax.broadcasted_iota(jnp.int32, (atoms, AW), 0) < count
+    mid_out[...] = jnp.where(live, mid, jnp.zeros_like(mid))
     lifted = jnp.maximum(mm(mid, lift[...]), 0.0).astype(BF16)
     member = jnp.where(membership(tok[...], count, tokens), 1.0, 0.0)
     summed = mm(member.astype(BF16), lifted)
     counts = jnp.sum(member, axis=1, keepdims=True)
-    copies[4].wait()
     hidden = tsingle[...].astype(F32) + summed / counts
     hidden_out[...] = hidden
     normed_out[...] = normalise(hidden, tgain[...])
@@ -205,7 +167,8 @@
 
 def query_body(info, normed, tok, qg, out, member_out, normed_out):
     tokens = normed.shape[0]
-    member = membership(tok[...], info[lax.axis_index("row")], tokens)
+    count = info[lax.axis_index("row")]
+    member = membership(tok[...], count, tokens)
     r = lax.broadcasted_iota(jnp.int32, (tokens, 3 * tokens), 0)
     c = lax.broadcasted_iota(jnp.int32, (tokens, 3 * tokens), 1)
     same = (c == r) | (c == r + tokens) | (c == r + 2 * tokens)
@@ -222,8 +185,8 @@
     if not begins:
         st_in, acc_in, *refs = refs
     if ends:
-        info, hidden_in, mid, member, proj_hbm, down, atom_out, token_out, *refs = refs
-        xs, kvs, qs, proj, sems = refs
+        hidden_in, base, member, proj, down, atom_out, token_out, *refs = refs
+        xs, kvs, qs, result, sems = refs
     else:
         st_out, acc_out, *refs = refs
         xs, kvs, qs = refs
@@ -232,9 +195,6 @@
     tokens = own[0].shape[0]
     pair = 2 * tokens
     keys = number * pair
-    if ends:
-        fetch = pltpu.make_async_copy(proj_hbm, proj, sems.at[0])
-        fetch.start()
     for j in range(number):
         at = pl.multiple_of(j * pair + core * tokens, tokens)
         xs[pl.ds(at, tokens), :] = own[j][...]
@@ -301,20 +261,19 @@
     if not ends:
         return
     attended = jnp.concatenate(pieces, axis=1)
-    count = info[row]
-    atoms = mid.shape[0]
     gated = (attended * sigmoid(query_gate[:, TW:].astype(F32))).astype(BF16)
-    fetch.wait()
     final = (hidden_in[...] + mm(gated, proj[...])).astype(BF16)
-    token_out[...] = final
+    result[...] = final
+    store = pltpu.make_async_copy(result, token_out, sems.at[0])
+    store.start()
     back = mm(final, down[...])
     high = back.astype(BF16)
     rest = back - high.astype(F32)
     low = rest.astype(BF16)
     lowest = (rest - low.astype(F32)).astype(BF16)
     spread = mm(member[...], jnp.concatenate([high, low, lowest], axis=0))
-    live = lax.broadcasted_iota(jnp.int32, (atoms, AW), 0) < count
-    atom_out[...] = jnp.where(live, mid[...].astype(F32) + spread, 0.0).astype(BF16)
+    atom_out[...] = (base[...].astype(F32) + spread).astype(BF16)
+    store.wait()
 
 
 def vmem(count):
@@ -358,48 +317,34 @@
         near = swap(atom_single, 1)
         tok = atom_token.reshape(1, atoms)
         gain = atom_gain.reshape(1, AW)
-        q, kv, gate, att = pl.pallas_call(
+        q, kv, gate, gated = pl.pallas_call(
             early_body,
             out_shape=(
                 like((atoms, AW), BF16), like((rows, 2 * AW), BF16), like((atoms, AW), BF16),
-                like((atoms, AW), F32),
+                like((atoms, AW), BF16),
             ),
-            in_specs=scalars() + anywhere(2) + vmem(1) + anywhere(1),
+            in_specs=scalars() + vmem(4),
             out_specs=tuple(vmem(4)),
-            scratch_shapes=[
-                VMEM((atoms, AW), BF16), VMEM(atom_bias.shape, BF16), VMEM((AW, 4 * AW), BF16),
-                pltpu.SemaphoreType.DMA((4,)),
-            ],
-            cost_estimate=pl.CostEstimate(
-                flops=2 * atoms * AW * (4 * AW + 3 * WK * AH), transcendentals=atoms * AH * WK,
-                bytes_accessed=8 << 20,
-            ),
+            compiler_params=pltpu.CompilerParams(vmem_limit_bytes=59200 << 10),
             name="early",
         )(atom_count, atom_single, atom_bias, gain, atom_qkvg)
         normed, hidden, mid = pl.pallas_call(
             late_body,
             out_shape=(like((tokens, TW), BF16), like((tokens, TW), F32), like((atoms, AW), BF16)),
-            in_specs=scalars() + vmem(9) + anywhere(6),
+            in_specs=scalars() + vmem(15),
             out_specs=tuple(vmem(3)),
-            scratch_shapes=[
-                VMEM((rows, 2 * AW), BF16), VMEM((atoms, AW), F32),
-                VMEM((5, AH, WQ, WK), BF16), VMEM((AW, 2 * AW), BF16), VMEM((atoms, AW), BF16),
-                VMEM((AW, AW), BF16), VMEM((AW, TW), BF16), VMEM((tokens, TW), BF16),
-                pltpu.SemaphoreType.DMA((7,)),
-            ],
+            scratch_shapes=[VMEM((rows, 2 * AW), BF16), VMEM((atoms, AW), BF16)],
             compiler_params=pltpu.CompilerParams(vmem_limit_bytes=59200 << 10),
-            cost_estimate=pl.CostEstimate(
-                flops=4 * atoms * AW * TW, transcendentals=atoms * AH * WK, bytes_accessed=8 << 20,
-            ),
             name="late",
         )(
-            atom_count, near, far, q, kv, gate, att, tok, gain, token_gain, atom_bias,
+            atom_count, near, far, q, kv, gate, gated, tok, gain, token_gain, atom_bias,
             atom_qkvg, atom_single, atom_proj, atom_to_token, token_single,
         )
         blocks, other = {0: normed}, {}
         for k in range(1, nchip):
             top = 1 << (k.bit_length() - 1)
-            blocks[k] = swap(normed if k == top else blocks[top], 2 * (k if k == top else k ^ top))
+            direct = k == top or k < 4
+            blocks[k] = swap(normed if direct else blocks[top], 2 * (k if direct else k ^ top))
         for k in range(nchip):
             other[k] = swap(blocks[k], 1)
         query_gate, member, normed_again = pl.pallas_call(
@@ -427,17 +372,17 @@
                 VMEM((keys, TW), BF16), VMEM((keys, 2 * TW), BF16), VMEM((TH * tokens, 256), BF16),
             ]
             if ends:
-                arrays += [atom_count, hidden, mid, member, token_proj, token_to_atom]
-                specs += scalars() + vmem(3) + anywhere(1) + vmem(1)
+                arrays += [hidden, mid, member, token_proj, token_to_atom]
+                specs += vmem(5)
                 outs = (like((atoms, AW), BF16), like((tokens, TW), BF16))
-                scratch += [VMEM((TW, TW), BF16), pltpu.SemaphoreType.DMA((1,))]
+                scratch += [VMEM((tokens, TW), BF16), pltpu.SemaphoreType.DMA((1,))]
             else:
                 outs = (like((TH * tokens, 128), F32), like((TH * tokens, 256), F32))
             state = pl.pallas_call(
                 lambda *refs: token_body(offsets, begins, ends, *refs),
                 out_shape=outs,
                 in_specs=specs,
-                out_specs=tuple(vmem(2)),
+                out_specs=tuple(vmem(1) + (anywhere(1) if ends else vmem(1))),
                 scratch_shapes=scratch,
                 compiler_params=pltpu.CompilerParams(vmem_limit_bytes=16 << 20),
             )(*arrays)

time: 47.6 us -> 42.9 us (0.901)
  waiting for transfers between devices: 10.5 us -> 6.78 us
  Pallas kernels: 18.1 us -> 15.9 us
  starting transfers between devices: 14.5 us -> 16 us
    ppermute x16, waiting for transfers between devices: 10.5 us -> 6.78 us  [swap(): return lax.ppermute(value, 'row', [(i, i ^ bits) for i in range(width)])]
    ppermute x16, starting transfers between devices: 13.9 us -> 15.3 us  [swap(): return lax.ppermute(value, 'row', [(i, i ^ bits) for i in range(width)])]
    pallas_call x1, Pallas kernels: 4.14 us -> 3.23 us  [on_device(): pl.pallas_call(early_body, out_shape=(like((atoms, AW), BF16), like((rows...]
    pallas_call x2, Pallas kernels: 7.53 us -> 6.85 us  [on_device(): pl.pallas_call(lambda *refs: token_body(offsets, begins, ends, *refs), ou...]
    pallas_call x1, Pallas kernels: 5.25 us -> 4.61 us  [on_device(): pl.pallas_call(late_body, out_shape=(like((tokens, TW), BF16), like((toke...]
  transfers between devices with their start and end apart: 17 -> 17, of which waited for: 6 -> 5; matrix products, arithmetic and copies ran while one was open for 0% -> 0% of each run, Pallas kernels for 17% -> 16%
where the time goes in v1:
time: 42.9 us; the launch traced here: 42.7 us
  starting transfers between devices  16 us (37%)
  Pallas kernels  15.9 us (37%)
  waiting for transfers between devices  6.78 us (16%)
  local copies, waits for them, and re-layouts  3.26 us (8%)
  between operations  0.83 us (2%)
    ppermute x16, starting transfers between devices, swap(): return lax.ppermute(value, 'row', [(i, i ^ bits) for i in range(width)])  15.3 us
    pallas_call x2, Pallas kernels, on_device(): pl.pallas_call(lambda *refs: token_body(offsets, begins, ends, *refs), ou...  6.85 us
    ppermute x16, waiting for transfers between devices, swap(): return lax.ppermute(value, 'row', [(i, i ^ bits) for i in range(width)])  6.78 us
    pallas_call x1, Pallas kernels, on_device(): pl.pallas_call(late_body, out_shape=(like((tokens, TW), BF16), like((toke...  4.61 us
    unnamed x24, local copies, waits for them, and re-layouts  3.26 us
    pallas_call x1, Pallas kernels, on_device(): pl.pallas_call(early_body, out_shape=(like((atoms, AW), BF16), like((rows...  3.23 us
    pallas_call x1, Pallas kernels, on_device(): pl.pallas_call(query_body, out_shape=(like((tokens, 2 * TW), BF16), like(...  1.19 us
  transfers between devices with their start and end apart: 17, of which 5 were waited for; matrix products, arithmetic and copies ran while one was open for 0% of the time, Pallas kernels for 16%

profile of v1, /device:TPU:0, one launch (start us, length us, event | category | flops | bytes accessed | tf_op | source)
XLA Modules:
  0.0 42.7 jit_solution(1241617932693623265)
XLA Ops:
  0.6 0.0 copy-start.9
  0.6 0.0 copy-start.8
  0.7 0.6 %collective-permute-start = (bf16[512,128]{1,0:T(8,128)(2,1)}, bf16[512,128]{1,0:T(8,128)(2,1)S(1)}, u32[]{:S(2)}, u32[]{:S(2)}) collective-permute-start(bf16[512,128]{1,0:T(8,128)(2,1)} %x.3), channel_id=1, source_target_pairs={{0,1},{1,0},{2,3},{3,2},{4,5},{5,4},{6,7},{7,6},{8,9},{9,8},{10,11... | collective-permute-start | bytes 393224 | tf_op jit(solution)/shard_map/ppermute | solution.py:303
  1.2 0.7 %collective-permute-start.1 = (bf16[512,128]{1,0:T(8,128)(2,1)}, bf16[512,128]{1,0:T(8,128)(2,1)S(1)}, u32[]{:S(2)}, u32[]{:S(2)}) collective-permute-start(bf16[512,128]{1,0:T(8,128)(2,1)} %x.3), channel_id=1, source_target_pairs={{1,2},{2,1},{3,4},{4,3},{5,6},{6,5},{7,8},{8,7},{9,10},{10,9},{11,... | collective-permute-start | bytes 393224 | tf_op jit(solution)/shard_map/ppermute | solution.py:313
  1.9 3.2 %early.1 = (bf16[512,128]{1,0:T(8,128)(2,1)}, bf16[640,256]{1,0:T(8,128)(2,1)}, bf16[512,128]{1,0:T(8,128)(2,1)}, bf16[512,128]{1,0:T(8,128)(2,1)}) custom-call(s32[16]{0:T(128)} %info.5, bf16[512,128]{1,0:T(8,128)(2,1)} %x.3, bf16[16,4,32,128]{3,2,1,0:T(8,128)(2,1)} %bias.3, f32[1,128]{1,0:T(1,128)} %bitcast.4, bf16[128,512]{1,0:T(8,128)(2,1)} %qkvg.3), custom_call_target="tpu_custom_call" | custom-call | tf_op jit(solution)/shard_map/early/pallas_call | solution.py:320
  5.1 0.0 copy-start
  5.1 0.0 copy-start.1
  5.1 0.0 collective-permute-done.near
  5.1 0.0 copy-start.10
  5.1 0.0 collective-permute-done.1.far
  5.1 0.0 copy-start.11
  5.1 0.6 %copy-done.10 = bf16[512,128]{1,0:T(8,128)(2,1)} copy-done((bf16[512,128]{1,0:T(8,128)(2,1)}, bf16[512,128]{1,0:T(8,128)(2,1)S(1)}, u32[]{:S(2)}) %copy-start.10) | copy-done | bytes 131096
  5.8 0.0 copy-done.11
  5.8 4.6 %late.1 = (bf16[64,768]{1,0:T(8,128)(2,1)}, f32[64,768]{1,0:T(8,128)}, bf16[512,128]{1,0:T(8,128)(2,1)}) custom-call(s32[16]{0:T(128)} %info.5, bf16[512,128]{1,0:T(8,128)(2,1)} %copy-done.10, bf16[512,128]{1,0:T(8,128)(2,1)} %copy-done.11, bf16[512,128]{1,0:T(8,128)(2,1)} %get-tuple-element.14.q, bf16[640,256]{1,0:T(8,128)(2,1)} %get-tuple-element.15.kv_in, ...), custom_call_target="tpu_custom_call" | custom-call | tf_op jit(solution)/shard_map/late/pallas_call | solution.py:331
  10.4 6.7 %collective-permute-start.3 = (bf16[64,768]{1,0:T(8,128)(2,1)}, bf16[64,768]{1,0:T(8,128)(2,1)S(1)}, u32[]{:S(2)}, u32[]{:S(2)}) collective-permute-start(bf16[64,768]{1,0:T(8,128)(2,1)} %get-tuple-element.18.normed), channel_id=1, source_target_pairs={{0,8},{1,9},{2,10},{3,11},{4,12},{5,13},{6,14},{7,15},{8,0},{9,1},... | collective-permute-start | bytes 294920 | tf_op jit(solution)/shard_map/ppermute | solution.py:303
  17.1 0.7 %collective-permute-start.11 = (bf16[64,768]{1,0:T(8,128)(2,1)}, bf16[64,768]{1,0:T(8,128)(2,1)S(1)}, u32[]{:S(2)}, u32[]{:S(2)}) collective-permute-start(bf16[64,768]{1,0:T(8,128)(2,1)} %get-tuple-element.18.normed), channel_id=1, source_target_pairs={{0,2},{1,3},{2,0},{3,1},{4,6},{5,7},{6,4},{7,5},{8,10},{9,11},{10,... | collective-permute-start | bytes 294920 | tf_op jit(solution)/shard_map/ppermute | solution.py:303
  17.8 1.6 %collective-permute-start.12 = (bf16[64,768]{1,0:T(8,128)(2,1)}, bf16[64,768]{1,0:T(8,128)(2,1)S(1)}, u32[]{:S(2)}, u32[]{:S(2)}) collective-permute-start(bf16[64,768]{1,0:T(8,128)(2,1)} %get-tuple-element.18.normed), channel_id=1, source_target_pairs={{0,4},{1,5},{2,6},{3,7},{4,0},{5,1},{6,2},{7,3},{8,12},{9,13},{10,... | collective-permute-start | bytes 294920 | tf_op jit(solution)/shard_map/ppermute | solution.py:303
  19.4 0.0 collective-permute-start.13
  19.4 1.2 %collective-permute-start.2 = (bf16[64,768]{1,0:T(8,128)(2,1)}, bf16[64,768]{1,0:T(8,128)(2,1)S(1)}, u32[]{:S(2)}, u32[]{:S(2)}) collective-permute-start(bf16[64,768]{1,0:T(8,128)(2,1)} %get-tuple-element.18.normed), channel_id=1, source_target_pairs={{0,6},{1,7},{2,4},{3,5},{4,2},{5,3},{6,0},{7,1},{8,14},{9,15},{10,... | collective-permute-start | bytes 294920 | tf_op jit(solution)/shard_map/ppermute | solution.py:303
  20.7 2.3 %collective-permute-done.3.refs_3_ = bf16[64,768]{1,0:T(8,128)(2,1)S(1)} collective-permute-done((bf16[64,768]{1,0:T(8,128)(2,1)}, bf16[64,768]{1,0:T(8,128)(2,1)S(1)}, u32[]{:S(2)}, u32[]{:S(2)}) %collective-permute-start.3) | collective-permute-done | bytes 98336 | tf_op jit(solution)/shard_map/ppermute | solution.py:303
  23.0 0.0 collective-permute-start.16
  23.0 0.0 collective-permute-done.11.refs_1_
  23.0 0.5 %collective-permute-start.14 = (bf16[64,768]{1,0:T(8,128)(2,1)S(1)}, bf16[64,768]{1,0:T(8,128)(2,1)S(1)}, u32[]{:S(2)}, u32[]{:S(2)}) collective-permute-start(bf16[64,768]{1,0:T(8,128)(2,1)S(1)} %collective-permute-done.11.refs_1_), channel_id=1, source_target_pairs={{0,1},{1,0},{2,3},{3,2},{4,5},{5,4},{6,7},{7,6},{8,9},{9,8},{10,11... | collective-permute-start | bytes 294920 | tf_op jit(solution)/shard_map/ppermute | solution.py:303
  23.5 1.0 %collective-permute-done.12.refs_2_ = bf16[64,768]{1,0:T(8,128)(2,1)S(1)} collective-permute-done((bf16[64,768]{1,0:T(8,128)(2,1)}, bf16[64,768]{1,0:T(8,128)(2,1)S(1)}, u32[]{:S(2)}, u32[]{:S(2)}) %collective-permute-start.12) | collective-permute-done | bytes 98336 | tf_op jit(solution)/shard_map/ppermute | solution.py:303
  24.5 1.6 %collective-permute-start.6 = (bf16[64,768]{1,0:T(8,128)(2,1)S(1)}, bf16[64,768]{1,0:T(8,128)(2,1)S(1)}, u32[]{:S(2)}, u32[]{:S(2)}) collective-permute-start(bf16[64,768]{1,0:T(8,128)(2,1)S(1)} %collective-permute-done.3.refs_3_), channel_id=1, source_target_pairs={{0,6},{1,7},{2,4},{3,5},{4,2},{5,3},{6,0},{7,1},{8,14},{9,15},{10,... | collective-permute-start | bytes 294920 | tf_op jit(solution)/shard_map/ppermute | solution.py:303
  26.0 0.0 collective-permute-done.13.refs_4_
  26.0 0.7 %collective-permute-start.4 = (bf16[64,768]{1,0:T(8,128)(2,1)S(1)}, bf16[64,768]{1,0:T(8,128)(2,1)S(1)}, u32[]{:S(2)}, u32[]{:S(2)}) collective-permute-start(bf16[64,768]{1,0:T(8,128)(2,1)S(1)} %collective-permute-done.3.refs_3_), channel_id=1, source_target_pairs={{0,2},{1,3},{2,0},{3,1},{4,6},{5,7},{6,4},{7,5},{8,10},{9,11},{10,... | collective-permute-start | bytes 294920 | tf_op jit(solution)/shard_map/ppermute | solution.py:303
  26.8 0.0 collective-permute-done.2.refs_0_
  26.8 1.2 %collective-permute-start.5 = (bf16[64,768]{1,0:T(8,128)(2,1)S(1)}, bf16[64,768]{1,0:T(8,128)(2,1)S(1)}, u32[]{:S(2)}, u32[]{:S(2)}) collective-permute-start(bf16[64,768]{1,0:T(8,128)(2,1)S(1)} %collective-permute-done.3.refs_3_), channel_id=1, source_target_pairs={{0,4},{1,5},{2,6},{3,7},{4,0},{5,1},{6,2},{7,3},{8,12},{9,13},{10,... | collective-permute-start | bytes 294920 | tf_op jit(solution)/shard_map/ppermute | solution.py:303
  28.0 0.0 collective-permute-done.16.refs_7_
  28.0 0.0 collective-permute-start.15
  28.0 0.0 collective-permute-done.14.refs_5_
  28.0 0.5 %collective-permute-start.7 = (bf16[64,768]{1,0:T(8,128)(2,1)S(1)}, bf16[64,768]{1,0:T(8,128)(2,1)S(1)}, u32[]{:S(2)}, u32[]{:S(2)}) collective-permute-start(bf16[64,768]{1,0:T(8,128)(2,1)S(1)} %collective-permute-done.2.refs_0_), channel_id=1, source_target_pairs={{0,1},{1,0},{2,3},{3,2},{4,5},{5,4},{6,7},{7,6},{8,9},{9,8},{10,11... | collective-permute-start | bytes 294920 | tf_op jit(solution)/shard_map/ppermute | solution.py:303
  28.5 2.0 %collective-permute-done.6.refs_3_ = bf16[64,768]{1,0:T(8,128)(2,1)S(1)} collective-permute-done((bf16[64,768]{1,0:T(8,128)(2,1)S(1)}, bf16[64,768]{1,0:T(8,128)(2,1)S(1)}, u32[]{:S(2)}, u32[]{:S(2)}) %collective-permute-start.6) | collective-permute-done | bytes 98336 | tf_op jit(solution)/shard_map/ppermute | solution.py:303
  30.5 0.0 collective-permute-start.10
  30.5 0.9 %collective-permute-done.4.refs_1_ = bf16[64,768]{1,0:T(8,128)(2,1)S(1)} collective-permute-done((bf16[64,768]{1,0:T(8,128)(2,1)S(1)}, bf16[64,768]{1,0:T(8,128)(2,1)S(1)}, u32[]{:S(2)}, u32[]{:S(2)}) %collective-permute-start.4) | collective-permute-done | bytes 98336 | tf_op jit(solution)/shard_map/ppermute | solution.py:303
  31.4 0.0 collective-permute-start.8
  31.4 0.5 %collective-permute-done.5.refs_2_ = bf16[64,768]{1,0:T(8,128)(2,1)S(1)} collective-permute-done((bf16[64,768]{1,0:T(8,128)(2,1)S(1)}, bf16[64,768]{1,0:T(8,128)(2,1)S(1)}, u32[]{:S(2)}, u32[]{:S(2)}) %collective-permute-start.5) | collective-permute-done | bytes 98336 | tf_op jit(solution)/shard_map/ppermute | solution.py:303
  31.9 0.0 collective-permute-start.9
  31.9 0.0 copy-done.9
  31.9 0.0 copy-done.8
  32.0 0.0 copy-start.2
  32.0 1.7 %copy-done.2 = bf16[768,1536]{1,0:T(8,128)(2,1)S(1)} copy-done((bf16[768,1536]{1,0:T(8,128)(2,1)S(1)}, bf16[768,1536]{1,0:T(8,128)(2,1)}, u32[]{:S(2)}) %copy-start.2) | copy-done | bytes 2359320
  33.6 0.0 copy-start.7
  33.6 0.9 %copy-done.7 = bf16[64,768]{1,0:T(8,128)(2,1)S(1)} copy-done((bf16[64,768]{1,0:T(8,128)(2,1)S(1)}, bf16[64,768]{1,0:T(8,128)(2,1)}, u32[]{:S(2)}) %copy-start.7) | copy-done | bytes 98328
  34.5 1.2 %queries.1 = (bf16[64,1536]{1,0:T(8,128)(2,1)S(1)}, bf16[512,192]{1,0:T(8,128)(2,1)S(1)}, bf16[64,768]{1,0:T(8,128)(2,1)S(1)}) custom-call(s32[16]{0:T(128)S(1)} %copy-done.9, bf16[64,768]{1,0:T(8,128)(2,1)S(1)} %copy-done.7, s32[1,512]{1,0:T(1,128)S(1)} %bitcast.3, bf16[768,1536]{1,0:T(8,128)(2,1)S(1)} %copy-done.2), custom_call_target="tpu_custom_call" | custom-call | tf_op jit(solution)/shard_map/queries/pallas_call | solution.py:350
  35.7 0.0 collective-permute-done.15.refs_6_
  35.7 0.0 copy-done
  35.7 0.0 copy-done.1
  35.7 0.0 copy-start.3
  35.7 0.0 copy-start.4
  35.8 0.0 copy-start.5
  35.8 0.0 copy-start.6
  35.8 2.5 %shard_map.158 = (f32[1024,128]{1,0:T(8,128)S(1)}, f32[1024,256]{1,0:T(8,128)S(1)}) custom-call(bf16[64,768]{1,0:T(8,128)(2,1)S(1)} %get-tuple-element.20.refs_0_, bf16[64,768]{1,0:T(8,128)(2,1)S(1)} %collective-permute-done.11.refs_1_, bf16[64,768]{1,0:T(8,128)(2,1)S(1)} %collective-permute-done.12.refs_2_, ...), custom_call_target="tpu_custom_call" | custom-call | tf_op jit(solution)/shard_map/pallas_call | solution.py:381
  38.3 0.0 collective-permute-done.7.refs_4_
  38.3 0.0 collective-permute-done.10.refs_7_
  38.3 0.0 collective-permute-done.8.refs_5_
  38.3 0.0 collective-permute-done.9.refs_6_
  38.3 0.0 copy-done.3
  38.4 0.0 copy-done.4
  38.4 0.0 copy-done.5
  38.4 0.0 copy-done.6
  38.4 4.3 %shard_map.159 = (bf16[512,128]{1,0:T(8,128)(2,1)}, bf16[64,768]{1,0:T(8,128)(2,1)}) custom-call(bf16[64,768]{1,0:T(8,128)(2,1)S(1)} %collective-permute-done.2.refs_0_, bf16[64,768]{1,0:T(8,128)(2,1)S(1)} %collective-permute-done.4.refs_1_, bf16[64,768]{1,0:T(8,128)(2,1)S(1)} %collective-permute-done.5.refs_2_, ...), custom_call_target="tpu_custom_call" | custom-call | tf_op jit(solution)/shard_map/pallas_call | solution.py:381
Async XLA Ops:
  0.6 31.3 %copy-start.9 = (s32[16]{0:T(128)S(1)}, s32[16]{0:T(128)}, u32[]{:S(2)}) copy-start(s32[16]{0:T(128)} %info.5) | copy-start | bytes 196
  0.6 31.3 %copy-start.8 = (s32[512]{0:T(512)S(1)}, s32[512]{0:T(512)}, u32[]{:S(2)}) copy-start(s32[512]{0:T(512)} %param.17) | copy-start | bytes 6148
  0.7 4.5 %collective-permute-start = (bf16[512,128]{1,0:T(8,128)(2,1)}, bf16[512,128]{1,0:T(8,128)(2,1)S(1)}, u32[]{:S(2)}, u32[]{:S(2)}) collective-permute-start(bf16[512,128]{1,0:T(8,128)(2,1)} %x.3), channel_id=1, source_target_pairs={{0,1},{1,0},{2,3},{3,2},{4,5},{5,4},{6,7},{7,6},{8,9},{9,8},{10,11... | collective-permute-start | bytes 393224 | tf_op jit(solution)/shard_map/ppermute | solution.py:303
  1.2 3.9 %collective-permute-start.1 = (bf16[512,128]{1,0:T(8,128)(2,1)}, bf16[512,128]{1,0:T(8,128)(2,1)S(1)}, u32[]{:S(2)}, u32[]{:S(2)}) collective-permute-start(bf16[512,128]{1,0:T(8,128)(2,1)} %x.3), channel_id=1, source_target_pairs={{1,2},{2,1},{3,4},{4,3},{5,6},{6,5},{7,8},{8,7},{9,10},{10,9},{11,... | collective-permute-start | bytes 393224 | tf_op jit(solution)/shard_map/ppermute | solution.py:313
  5.1 30.6 %copy-start = (bf16[768,1536]{1,0:T(8,128)(2,1)S(1)}, bf16[768,1536]{1,0:T(8,128)(2,1)}, u32[]{:S(2)}) copy-start(bf16[768,1536]{1,0:T(8,128)(2,1)} %refs_9_.3) | copy-start | bytes 7077892
  5.1 30.6 %copy-start.1 = (bf16[16,64,1024]{2,1,0:T(8,128)(2,1)S(1)}, bf16[16,64,1024]{2,1,0:T(8,128)(2,1)}, u32[]{:S(2)}) copy-start(bf16[16,64,1024]{2,1,0:T(8,128)(2,1)} %refs_10_.3) | copy-start | bytes 6291460
  5.1 0.7 %copy-start.10 = (bf16[512,128]{1,0:T(8,128)(2,1)}, bf16[512,128]{1,0:T(8,128)(2,1)S(1)}, u32[]{:S(2)}) copy-start(bf16[512,128]{1,0:T(8,128)(2,1)S(1)} %collective-permute-done.near) | copy-start | bytes 393220
  5.1 0.7 %copy-start.11 = (bf16[512,128]{1,0:T(8,128)(2,1)}, bf16[512,128]{1,0:T(8,128)(2,1)S(1)}, u32[]{:S(2)}) copy-start(bf16[512,128]{1,0:T(8,128)(2,1)S(1)} %collective-permute-done.1.far) | copy-start | bytes 393220
  10.4 12.6 %collective-permute-start.3 = (bf16[64,768]{1,0:T(8,128)(2,1)}, bf16[64,768]{1,0:T(8,128)(2,1)S(1)}, u32[]{:S(2)}, u32[]{:S(2)}) collective-permute-start(bf16[64,768]{1,0:T(8,128)(2,1)} %get-tuple-element.18.normed), channel_id=1, source_target_pairs={{0,8},{1,9},{2,10},{3,11},{4,12},{5,13},{6,14},{7,15},{8,0},{9,1},... | collective-permute-start | bytes 294920 | tf_op jit(solution)/shard_map/ppermute | solution.py:303
  17.1 5.9 %collective-permute-start.11 = (bf16[64,768]{1,0:T(8,128)(2,1)}, bf16[64,768]{1,0:T(8,128)(2,1)S(1)}, u32[]{:S(2)}, u32[]{:S(2)}) collective-permute-start(bf16[64,768]{1,0:T(8,128)(2,1)} %get-tuple-element.18.normed), channel_id=1, source_target_pairs={{0,2},{1,3},{2,0},{3,1},{4,6},{5,7},{6,4},{7,5},{8,10},{9,11},{10,... | collective-permute-start | bytes 294920 | tf_op jit(solution)/shard_map/ppermute | solution.py:303
  17.8 6.6 %collective-permute-start.12 = (bf16[64,768]{1,0:T(8,128)(2,1)}, bf16[64,768]{1,0:T(8,128)(2,1)S(1)}, u32[]{:S(2)}, u32[]{:S(2)}) collective-permute-start(bf16[64,768]{1,0:T(8,128)(2,1)} %get-tuple-element.18.normed), channel_id=1, source_target_pairs={{0,4},{1,5},{2,6},{3,7},{4,0},{5,1},{6,2},{7,3},{8,12},{9,13},{10,... | collective-permute-start | bytes 294920 | tf_op jit(solution)/shard_map/ppermute | solution.py:303
  19.4 6.6 %collective-permute-start.13 = (bf16[64,768]{1,0:T(8,128)(2,1)}, bf16[64,768]{1,0:T(8,128)(2,1)S(1)}, u32[]{:S(2)}, u32[]{:S(2)}) collective-permute-start(bf16[64,768]{1,0:T(8,128)(2,1)} %get-tuple-element.18.normed), channel_id=1, source_target_pairs={{0,1},{1,0},{2,3},{3,2},{4,5},{5,4},{6,7},{7,6},{8,9},{9,8},{10,11... | collective-permute-start | bytes 294920 | tf_op jit(solution)/shard_map/ppermute | solution.py:303
  19.4 7.3 %collective-permute-start.2 = (bf16[64,768]{1,0:T(8,128)(2,1)}, bf16[64,768]{1,0:T(8,128)(2,1)S(1)}, u32[]{:S(2)}, u32[]{:S(2)}) collective-permute-start(bf16[64,768]{1,0:T(8,128)(2,1)} %get-tuple-element.18.normed), channel_id=1, source_target_pairs={{0,6},{1,7},{2,4},{3,5},{4,2},{5,3},{6,0},{7,1},{8,14},{9,15},{10,... | collective-permute-start | bytes 294920 | tf_op jit(solution)/shard_map/ppermute | solution.py:303
  23.0 5.0 %collective-permute-start.16 = (bf16[64,768]{1,0:T(8,128)(2,1)S(1)}, bf16[64,768]{1,0:T(8,128)(2,1)S(1)}, u32[]{:S(2)}, u32[]{:S(2)}) collective-permute-start(bf16[64,768]{1,0:T(8,128)(2,1)S(1)} %collective-permute-done.3.refs_3_), channel_id=1, source_target_pairs={{0,1},{1,0},{2,3},{3,2},{4,5},{5,4},{6,7},{7,6},{8,9},{9,8},{10,11... | collective-permute-start | bytes 294920 | tf_op jit(solution)/shard_map/ppermute | solution.py:303
  23.0 5.0 %collective-permute-start.14 = (bf16[64,768]{1,0:T(8,128)(2,1)S(1)}, bf16[64,768]{1,0:T(8,128)(2,1)S(1)}, u32[]{:S(2)}, u32[]{:S(2)}) collective-permute-start(bf16[64,768]{1,0:T(8,128)(2,1)S(1)} %collective-permute-done.11.refs_1_), channel_id=1, source_target_pairs={{0,1},{1,0},{2,3},{3,2},{4,5},{5,4},{6,7},{7,6},{8,9},{9,8},{10,11... | collective-permute-start | bytes 294920 | tf_op jit(solution)/shard_map/ppermute | solution.py:303
  24.5 6.0 %collective-permute-start.6 = (bf16[64,768]{1,0:T(8,128)(2,1)S(1)}, bf16[64,768]{1,0:T(8,128)(2,1)S(1)}, u32[]{:S(2)}, u32[]{:S(2)}) collective-permute-start(bf16[64,768]{1,0:T(8,128)(2,1)S(1)} %collective-permute-done.3.refs_3_), channel_id=1, source_target_pairs={{0,6},{1,7},{2,4},{3,5},{4,2},{5,3},{6,0},{7,1},{8,14},{9,15},{10,... | collective-permute-start | bytes 294920 | tf_op jit(solution)/shard_map/ppermute | solution.py:303
  26.0 5.4 %collective-permute-start.4 = (bf16[64,768]{1,0:T(8,128)(2,1)S(1)}, bf16[64,768]{1,0:T(8,128)(2,1)S(1)}, u32[]{:S(2)}, u32[]{:S(2)}) collective-permute-start(bf16[64,768]{1,0:T(8,128)(2,1)S(1)} %collective-permute-done.3.refs_3_), channel_id=1, source_target_pairs={{0,2},{1,3},{2,0},{3,1},{4,6},{5,7},{6,4},{7,5},{8,10},{9,11},{10,... | collective-permute-start | bytes 294920 | tf_op jit(solution)/shard_map/ppermute | solution.py:303
  26.8 5.2 %collective-permute-start.5 = (bf16[64,768]{1,0:T(8,128)(2,1)S(1)}, bf16[64,768]{1,0:T(8,128)(2,1)S(1)}, u32[]{:S(2)}, u32[]{:S(2)}) collective-permute-start(bf16[64,768]{1,0:T(8,128)(2,1)S(1)} %collective-permute-done.3.refs_3_), channel_id=1, source_target_pairs={{0,4},{1,5},{2,6},{3,7},{4,0},{5,1},{6,2},{7,3},{8,12},{9,13},{10,... | collective-permute-start | bytes 294920 | tf_op jit(solution)/shard_map/ppermute | solution.py:303
  28.0 7.7 %collective-permute-start.15 = (bf16[64,768]{1,0:T(8,128)(2,1)S(1)}, bf16[64,768]{1,0:T(8,128)(2,1)S(1)}, u32[]{:S(2)}, u32[]{:S(2)}) collective-permute-start(bf16[64,768]{1,0:T(8,128)(2,1)S(1)} %collective-permute-done.12.refs_2_), channel_id=1, source_target_pairs={{0,1},{1,0},{2,3},{3,2},{4,5},{5,4},{6,7},{7,6},{8,9},{9,8},{10,11... | collective-permute-start | bytes 294920 | tf_op jit(solution)/shard_map/ppermute | solution.py:303
  28.0 10.3 %collective-permute-start.7 = (bf16[64,768]{1,0:T(8,128)(2,1)S(1)}, bf16[64,768]{1,0:T(8,128)(2,1)S(1)}, u32[]{:S(2)}, u32[]{:S(2)}) collective-permute-start(bf16[64,768]{1,0:T(8,128)(2,1)S(1)} %collective-permute-done.2.refs_0_), channel_id=1, source_target_pairs={{0,1},{1,0},{2,3},{3,2},{4,5},{5,4},{6,7},{7,6},{8,9},{9,8},{10,11... | collective-permute-start | bytes 294920 | tf_op jit(solution)/shard_map/ppermute | solution.py:303
  30.5 7.8 %collective-permute-start.10 = (bf16[64,768]{1,0:T(8,128)(2,1)S(1)}, bf16[64,768]{1,0:T(8,128)(2,1)S(1)}, u32[]{:S(2)}, u32[]{:S(2)}) collective-permute-start(bf16[64,768]{1,0:T(8,128)(2,1)S(1)} %collective-permute-done.6.refs_3_), channel_id=1, source_target_pairs={{0,1},{1,0},{2,3},{3,2},{4,5},{5,4},{6,7},{7,6},{8,9},{9,8},{10,11... | collective-permute-start | bytes 294920 | tf_op jit(solution)/shard_map/ppermute | solution.py:303
  31.4 6.9 %collective-permute-start.8 = (bf16[64,768]{1,0:T(8,128)(2,1)S(1)}, bf16[64,768]{1,0:T(8,128)(2,1)S(1)}, u32[]{:S(2)}, u32[]{:S(2)}) collective-permute-start(bf16[64,768]{1,0:T(8,128)(2,1)S(1)} %collective-permute-done.4.refs_1_), channel_id=1, source_target_pairs={{0,1},{1,0},{2,3},{3,2},{4,5},{5,4},{6,7},{7,6},{8,9},{9,8},{10,11... | collective-permute-start | bytes 294920 | tf_op jit(solution)/shard_map/ppermute | solution.py:303
  31.9 6.4 %collective-permute-start.9 = (bf16[64,768]{1,0:T(8,128)(2,1)S(1)}, bf16[64,768]{1,0:T(8,128)(2,1)S(1)}, u32[]{:S(2)}, u32[]{:S(2)}) collective-permute-start(bf16[64,768]{1,0:T(8,128)(2,1)S(1)} %collective-permute-done.5.refs_2_), channel_id=1, source_target_pairs={{0,1},{1,0},{2,3},{3,2},{4,5},{5,4},{6,7},{7,6},{8,9},{9,8},{10,11... | collective-permute-start | bytes 294920 | tf_op jit(solution)/shard_map/ppermute | solution.py:303
  32.0 1.7 %copy-start.2 = (bf16[768,1536]{1,0:T(8,128)(2,1)S(1)}, bf16[768,1536]{1,0:T(8,128)(2,1)}, u32[]{:S(2)}) copy-start(bf16[768,1536]{1,0:T(8,128)(2,1)} %qg.1) | copy-start | bytes 7077892
  33.6 0.9 %copy-start.7 = (bf16[64,768]{1,0:T(8,128)(2,1)S(1)}, bf16[64,768]{1,0:T(8,128)(2,1)}, u32[]{:S(2)}) copy-start(bf16[64,768]{1,0:T(8,128)(2,1)} %get-tuple-element.18.normed) | copy-start | bytes 294916
  35.7 2.6 %copy-start.3 = (bf16[768,768]{1,0:T(8,128)(2,1)S(1)}, bf16[768,768]{1,0:T(8,128)(2,1)}, u32[]{:S(2)}) copy-start(bf16[768,768]{1,0:T(8,128)(2,1)} %refs_16_.1) | copy-start | bytes 3538948
  35.7 2.6 %copy-start.4 = (bf16[768,128]{1,0:T(8,128)(2,1)S(1)}, bf16[768,128]{1,0:T(8,128)(2,1)}, u32[]{:S(2)}) copy-start(bf16[768,128]{1,0:T(8,128)(2,1)} %refs_17_.1) | copy-start | bytes 589828
  35.8 2.6 %copy-start.5 = (f32[64,768]{1,0:T(8,128)S(1)}, f32[64,768]{1,0:T(8,128)}, u32[]{:S(2)}) copy-start(f32[64,768]{1,0:T(8,128)} %get-tuple-element.23.refs_13_) | copy-start | bytes 589828
  35.8 2.6 %copy-start.6 = (bf16[512,128]{1,0:T(8,128)(2,1)S(1)}, bf16[512,128]{1,0:T(8,128)(2,1)}, u32[]{:S(2)}) copy-start(bf16[512,128]{1,0:T(8,128)(2,1)} %get-tuple-element.24.refs_14_) | copy-start | bytes 393220

commit v2 on v1

--- a/solution.py
+++ b/solution.py
@@ -73,7 +73,9 @@
     return out
 
 
-def early_body(info, x, bias, gain, qkvg, q_out, kv_out, gate_out, gated_out):
+def early_body(
+    info, x, bias, gain, qkvg, kv_out, gated_out, q_some, gate_some, bias_some, q_out, gate_out
+):
     row = lax.axis_index("row")
     count = info[row]
     atoms = x.shape[0]
@@ -92,6 +94,13 @@
             bias[w], WQ * w - LEFT_RIM, 0, count,
         )
         gated_out[own, :] = (out * sigmoid(gate_out[own, :].astype(F32))).astype(BF16)
+    last = (count - 1) // WQ
+    for w in range(5):
+        place = w if w < 2 else last + (w - 4)
+        own, to = pl.ds(pl.multiple_of(place * WQ, WQ), WQ), slice(WQ * w, WQ * (w + 1))
+        q_some[to, :] = q_out[own, :]
+        gate_some[to, :] = gate_out[own, :]
+        bias_some[w] = bias[place]
 
 
 def late_body(
@@ -129,16 +138,15 @@
     local = jnp.where((r >= 0) & (r < RIGHT_RIM), moved, local).astype(BF16)
     for w in range(5):
         if w < 2:
-            at, base, source, bias_at = WQ * w, WQ * w, kv, w
+            at, base, source = WQ * w, WQ * w, kv
         else:
             at = pl.multiple_of(start + WQ * (w - 2), WQ)
-            base, source, bias_at = WQ * (w - 2), local, last + (w - 4)
-        rows, own = slice(base, base + WK), pl.ds(at, WQ)
+            base, source = WQ * (w - 2), local
+        rows, own, to = slice(base, base + WK), pl.ds(at, WQ), slice(WQ * w, WQ * (w + 1))
         out = attend_window(
-            q[own, :], source[rows, :AW], source[rows, AW:], bias[bias_at], at - LEFT_RIM, low,
-            high,
-        )
-        gated[own, :] = (out * sigmoid(gate_in[own, :].astype(F32))).astype(BF16)
+            q[to, :], source[rows, :AW], source[rows, AW:], bias[w], at - LEFT_RIM, low, high,
+        )
+        gated[own, :] = (out * sigmoid(gate_in[to, :].astype(F32))).astype(BF16)
     mid = (x[...].astype(F32) + mm(gated[...], proj[...])).astype(BF16)
     live = lax.broadcasted_iota(jnp.int32, (atoms, AW), 0) < count
     mid_out[...] = jnp.where(live, mid, jnp.zeros_like(mid))
@@ -317,14 +325,15 @@
         near = swap(atom_single, 1)
         tok = atom_token.reshape(1, atoms)
         gain = atom_gain.reshape(1, AW)
-        q, kv, gate, gated = pl.pallas_call(
+        kv, gated, q, gate, some = pl.pallas_call(
             early_body,
             out_shape=(
-                like((atoms, AW), BF16), like((rows, 2 * AW), BF16), like((atoms, AW), BF16),
-                like((atoms, AW), BF16),
+                like((rows, 2 * AW), BF16), like((atoms, AW), BF16), like((5 * WQ, AW), BF16),
+                like((5 * WQ, AW), BF16), like((5, AH, WQ, WK), BF16),
             ),
             in_specs=scalars() + vmem(4),
-            out_specs=tuple(vmem(4)),
+            out_specs=tuple(vmem(5)),
+            scratch_shapes=[VMEM((atoms, AW), BF16), VMEM((atoms, AW), BF16)],
             compiler_params=pltpu.CompilerParams(vmem_limit_bytes=59200 << 10),
             name="early",
         )(atom_count, atom_single, atom_bias, gain, atom_qkvg)
@@ -337,7 +346,7 @@
             compiler_params=pltpu.CompilerParams(vmem_limit_bytes=59200 << 10),
             name="late",
         )(
-            atom_count, near, far, q, kv, gate, gated, tok, gain, token_gain, atom_bias,
+            atom_count, near, far, q, kv, gate, gated, tok, gain, token_gain, some,
             atom_qkvg, atom_single, atom_proj, atom_to_token, token_single,
         )
         blocks, other = {0: normed}, {}

time: 42.9 us -> 43.5 us (1.014)
  local copies, waits for them, and re-layouts: 3.26 us -> 3.95 us
  Pallas kernels: 15.9 us -> 15.4 us
    unnamed x24, local copies, waits for them, and re-layouts: 3.26 us -> 3.95 us
    pallas_call x1, Pallas kernels: 4.61 us -> 4.01 us  [on_device(): pl.pallas_call(late_body, out_shape=(like((tokens, TW), BF16), like((toke...]
where the time goes in v2:
time: 43.5 us; the launch traced here: 43.2 us
  starting transfers between devices  16.2 us (37%)
  Pallas kernels  15.4 us (35%)
  waiting for transfers between devices  6.78 us (16%)
  local copies, waits for them, and re-layouts  3.95 us (9%)
  between operations  0.82 us (2%)
    ppermute x16, starting transfers between devices, swap(): return lax.ppermute(value, 'row', [(i, i ^ bits) for i in range(width)])  15.6 us
    pallas_call x2, Pallas kernels, on_device(): pl.pallas_call(lambda *refs: token_body(offsets, begins, ends, *refs), ou...  6.85 us
    ppermute x16, waiting for transfers between devices, swap(): return lax.ppermute(value, 'row', [(i, i ^ bits) for i in range(width)])  6.78 us
    pallas_call x1, Pallas kernels, on_device(): pl.pallas_call(late_body, out_shape=(like((tokens, TW), BF16), like((toke...  4.01 us
    unnamed x24, local copies, waits for them, and re-layouts  3.95 us
    pallas_call x1, Pallas kernels, on_device(): pl.pallas_call(early_body, out_shape=(like((rows, 2 * AW), BF16), like((a...  3.39 us
    pallas_call x1, Pallas kernels, on_device(): pl.pallas_call(query_body, out_shape=(like((tokens, 2 * TW), BF16), like(...  1.18 us
  transfers between devices with their start and end apart: 17, of which 5 were waited for; matrix products, arithmetic and copies ran while one was open for 0% of the time, Pallas kernels for 16%

profile of v2, /device:TPU:0, one launch (start us, length us, event | category | flops | bytes accessed | tf_op | source)
XLA Modules:
  0.0 43.2 jit_solution(11986002749215128362)
XLA Ops:
  0.6 0.0 copy-start.9
  0.6 0.6 %collective-permute-start = (bf16[512,128]{1,0:T(8,128)(2,1)}, bf16[512,128]{1,0:T(8,128)(2,1)S(1)}, u32[]{:S(2)}, u32[]{:S(2)}) collective-permute-start(bf16[512,128]{1,0:T(8,128)(2,1)} %x.3), channel_id=1, source_target_pairs={{0,1},{1,0},{2,3},{3,2},{4,5},{5,4},{6,7},{7,6},{8,9},{9,8},{10,11... | collective-permute-start | bytes 393224 | tf_op jit(solution)/shard_map/ppermute | solution.py:311
  1.2 0.7 %collective-permute-start.1 = (bf16[512,128]{1,0:T(8,128)(2,1)}, bf16[512,128]{1,0:T(8,128)(2,1)S(1)}, u32[]{:S(2)}, u32[]{:S(2)}) collective-permute-start(bf16[512,128]{1,0:T(8,128)(2,1)} %x.3), channel_id=1, source_target_pairs={{1,2},{2,1},{3,4},{4,3},{5,6},{6,5},{7,8},{8,7},{9,10},{10,9},{11,... | collective-permute-start | bytes 393224 | tf_op jit(solution)/shard_map/ppermute | solution.py:321
  1.9 0.0 copy-start
  1.9 0.0 copy-start.1
  1.9 3.4 %early.1 = (bf16[640,256]{1,0:T(8,128)(2,1)}, bf16[512,128]{1,0:T(8,128)(2,1)}, bf16[160,128]{1,0:T(8,128)(2,1)}, bf16[160,128]{1,0:T(8,128)(2,1)}, bf16[5,4,32,128]{3,2,1,0:T(8,128)(2,1)}) custom-call(s32[16]{0:T(128)} %info.5, bf16[512,128]{1,0:T(8,128)(2,1)} %x.3, bf16[16,4,32,128]{3,2,1,0:T(8,128)(2,1)} %bias.1, f32[1,128]{1,0:T(1,128)} %bitcast.4, ...), custom_call_target="tpu_custom_call" | custom-call | tf_op jit(solution)/shard_map/early/pallas_call | solution.py:328
  5.3 0.0 collective-permute-done.near
  5.3 0.0 copy-start.10
  5.3 0.0 collective-permute-done.1.far
  5.3 0.0 copy-start.11
  5.3 0.6 %copy-done.10 = bf16[512,128]{1,0:T(8,128)(2,1)} copy-done((bf16[512,128]{1,0:T(8,128)(2,1)}, bf16[512,128]{1,0:T(8,128)(2,1)S(1)}, u32[]{:S(2)}) %copy-start.10) | copy-done | bytes 131096
  5.9 0.0 copy-done.11
  6.0 4.0 %late.1 = (bf16[64,768]{1,0:T(8,128)(2,1)}, f32[64,768]{1,0:T(8,128)}, bf16[512,128]{1,0:T(8,128)(2,1)}) custom-call(s32[16]{0:T(128)} %info.5, bf16[512,128]{1,0:T(8,128)(2,1)} %copy-done.10, bf16[512,128]{1,0:T(8,128)(2,1)} %copy-done.11, bf16[160,128]{1,0:T(8,128)(2,1)} %get-tuple-element.15.q, bf16[640,256]{1,0:T(8,128)(2,1)} %get-tuple-element.16.kv_in, ...), custom_call_target="tpu_custom_call" | custom-call | tf_op jit(solution)/shard_map/late/pallas_call | solution.py:340
  10.0 7.0 %collective-permute-start.3 = (bf16[64,768]{1,0:T(8,128)(2,1)}, bf16[64,768]{1,0:T(8,128)(2,1)S(1)}, u32[]{:S(2)}, u32[]{:S(2)}) collective-permute-start(bf16[64,768]{1,0:T(8,128)(2,1)} %get-tuple-element.20.normed), channel_id=1, source_target_pairs={{0,8},{1,9},{2,10},{3,11},{4,12},{5,13},{6,14},{7,15},{8,0},{9,1},... | collective-permute-start | bytes 294920 | tf_op jit(solution)/shard_map/ppermute | solution.py:311
  17.0 0.7 %collective-permute-start.11 = (bf16[64,768]{1,0:T(8,128)(2,1)}, bf16[64,768]{1,0:T(8,128)(2,1)S(1)}, u32[]{:S(2)}, u32[]{:S(2)}) collective-permute-start(bf16[64,768]{1,0:T(8,128)(2,1)} %get-tuple-element.20.normed), channel_id=1, source_target_pairs={{0,2},{1,3},{2,0},{3,1},{4,6},{5,7},{6,4},{7,5},{8,10},{9,11},{10,... | collective-permute-start | bytes 294920 | tf_op jit(solution)/shard_map/ppermute | solution.py:311
  17.7 1.6 %collective-permute-start.12 = (bf16[64,768]{1,0:T(8,128)(2,1)}, bf16[64,768]{1,0:T(8,128)(2,1)S(1)}, u32[]{:S(2)}, u32[]{:S(2)}) collective-permute-start(bf16[64,768]{1,0:T(8,128)(2,1)} %get-tuple-element.20.normed), channel_id=1, source_target_pairs={{0,4},{1,5},{2,6},{3,7},{4,0},{5,1},{6,2},{7,3},{8,12},{9,13},{10,... | collective-permute-start | bytes 294920 | tf_op jit(solution)/shard_map/ppermute | solution.py:311
  19.2 0.0 collective-permute-start.13
  19.2 1.2 %collective-permute-start.2 = (bf16[64,768]{1,0:T(8,128)(2,1)}, bf16[64,768]{1,0:T(8,128)(2,1)S(1)}, u32[]{:S(2)}, u32[]{:S(2)}) collective-permute-start(bf16[64,768]{1,0:T(8,128)(2,1)} %get-tuple-element.20.normed), channel_id=1, source_target_pairs={{0,6},{1,7},{2,4},{3,5},{4,2},{5,3},{6,0},{7,1},{8,14},{9,15},{10,... | collective-permute-start | bytes 294920 | tf_op jit(solution)/shard_map/ppermute | solution.py:311
  20.5 2.3 %collective-permute-done.3.refs_3_ = bf16[64,768]{1,0:T(8,128)(2,1)S(1)} collective-permute-done((bf16[64,768]{1,0:T(8,128)(2,1)}, bf16[64,768]{1,0:T(8,128)(2,1)S(1)}, u32[]{:S(2)}, u32[]{:S(2)}) %collective-permute-start.3) | collective-permute-done | bytes 98336 | tf_op jit(solution)/shard_map/ppermute | solution.py:311
  22.8 0.0 collective-permute-start.16
  22.8 0.0 collective-permute-done.11.refs_1_
  22.8 0.5 %collective-permute-start.14 = (bf16[64,768]{1,0:T(8,128)(2,1)S(1)}, bf16[64,768]{1,0:T(8,128)(2,1)S(1)}, u32[]{:S(2)}, u32[]{:S(2)}) collective-permute-start(bf16[64,768]{1,0:T(8,128)(2,1)S(1)} %collective-permute-done.11.refs_1_), channel_id=1, source_target_pairs={{0,1},{1,0},{2,3},{3,2},{4,5},{5,4},{6,7},{7,6},{8,9},{9,8},{10,11... | collective-permute-start | bytes 294920 | tf_op jit(solution)/shard_map/ppermute | solution.py:311
  23.3 1.0 %collective-permute-done.12.refs_2_ = bf16[64,768]{1,0:T(8,128)(2,1)S(1)} collective-permute-done((bf16[64,768]{1,0:T(8,128)(2,1)}, bf16[64,768]{1,0:T(8,128)(2,1)S(1)}, u32[]{:S(2)}, u32[]{:S(2)}) %collective-permute-start.12) | collective-permute-done | bytes 98336 | tf_op jit(solution)/shard_map/ppermute | solution.py:311
  24.3 1.6 %collective-permute-start.6 = (bf16[64,768]{1,0:T(8,128)(2,1)S(1)}, bf16[64,768]{1,0:T(8,128)(2,1)S(1)}, u32[]{:S(2)}, u32[]{:S(2)}) collective-permute-start(bf16[64,768]{1,0:T(8,128)(2,1)S(1)} %collective-permute-done.3.refs_3_), channel_id=1, source_target_pairs={{0,6},{1,7},{2,4},{3,5},{4,2},{5,3},{6,0},{7,1},{8,14},{9,15},{10,... | collective-permute-start | bytes 294920 | tf_op jit(solution)/shard_map/ppermute | solution.py:311
  25.9 0.0 collective-permute-done.13.refs_4_
  25.9 0.7 %collective-permute-start.4 = (bf16[64,768]{1,0:T(8,128)(2,1)S(1)}, bf16[64,768]{1,0:T(8,128)(2,1)S(1)}, u32[]{:S(2)}, u32[]{:S(2)}) collective-permute-start(bf16[64,768]{1,0:T(8,128)(2,1)S(1)} %collective-permute-done.3.refs_3_), channel_id=1, source_target_pairs={{0,2},{1,3},{2,0},{3,1},{4,6},{5,7},{6,4},{7,5},{8,10},{9,11},{10,... | collective-permute-start | bytes 294920 | tf_op jit(solution)/shard_map/ppermute | solution.py:311
  26.6 0.0 collective-permute-done.2.refs_0_
  26.6 1.2 %collective-permute-start.5 = (bf16[64,768]{1,0:T(8,128)(2,1)S(1)}, bf16[64,768]{1,0:T(8,128)(2,1)S(1)}, u32[]{:S(2)}, u32[]{:S(2)}) collective-permute-start(bf16[64,768]{1,0:T(8,128)(2,1)S(1)} %collective-permute-done.3.refs_3_), channel_id=1, source_target_pairs={{0,4},{1,5},{2,6},{3,7},{4,0},{5,1},{6,2},{7,3},{8,12},{9,13},{10,... | collective-permute-start | bytes 294920 | tf_op jit(solution)/shard_map/ppermute | solution.py:311
  27.8 0.0 collective-permute-done.16.refs_7_
  27.8 0.0 collective-permute-start.15
  27.8 0.0 collective-permute-done.14.refs_5_
  27.8 0.5 %collective-permute-start.7 = (bf16[64,768]{1,0:T(8,128)(2,1)S(1)}, bf16[64,768]{1,0:T(8,128)(2,1)S(1)}, u32[]{:S(2)}, u32[]{:S(2)}) collective-permute-start(bf16[64,768]{1,0:T(8,128)(2,1)S(1)} %collective-permute-done.2.refs_0_), channel_id=1, source_target_pairs={{0,1},{1,0},{2,3},{3,2},{4,5},{5,4},{6,7},{7,6},{8,9},{9,8},{10,11... | collective-permute-start | bytes 294920 | tf_op jit(solution)/shard_map/ppermute | solution.py:311
  28.3 2.0 %collective-permute-done.6.refs_3_ = bf16[64,768]{1,0:T(8,128)(2,1)S(1)} collective-permute-done((bf16[64,768]{1,0:T(8,128)(2,1)S(1)}, bf16[64,768]{1,0:T(8,128)(2,1)S(1)}, u32[]{:S(2)}, u32[]{:S(2)}) %collective-permute-start.6) | collective-permute-done | bytes 98336 | tf_op jit(solution)/shard_map/ppermute | solution.py:311
  30.3 0.0 collective-permute-start.10
  30.3 0.9 %collective-permute-done.4.refs_1_ = bf16[64,768]{1,0:T(8,128)(2,1)S(1)} collective-permute-done((bf16[64,768]{1,0:T(8,128)(2,1)S(1)}, bf16[64,768]{1,0:T(8,128)(2,1)S(1)}, u32[]{:S(2)}, u32[]{:S(2)}) %collective-permute-start.4) | collective-permute-done | bytes 98336 | tf_op jit(solution)/shard_map/ppermute | solution.py:311
  31.2 0.0 collective-permute-start.8
  31.2 0.5 %collective-permute-done.5.refs_2_ = bf16[64,768]{1,0:T(8,128)(2,1)S(1)} collective-permute-done((bf16[64,768]{1,0:T(8,128)(2,1)S(1)}, bf16[64,768]{1,0:T(8,128)(2,1)S(1)}, u32[]{:S(2)}, u32[]{:S(2)}) %collective-permute-start.5) | collective-permute-done | bytes 98336 | tf_op jit(solution)/shard_map/ppermute | solution.py:311
  31.8 0.0 collective-permute-start.9
  31.8 0.0 copy-done.9
  31.8 0.0 copy-start.2
  31.8 1.7 %copy-done.2 = bf16[768,1536]{1,0:T(8,128)(2,1)S(1)} copy-done((bf16[768,1536]{1,0:T(8,128)(2,1)S(1)}, bf16[768,1536]{1,0:T(8,128)(2,1)}, u32[]{:S(2)}) %copy-start.2) | copy-done | bytes 2359320
  33.4 0.0 copy-start.7
  33.5 0.9 %copy-done.7 = bf16[64,768]{1,0:T(8,128)(2,1)S(1)} copy-done((bf16[64,768]{1,0:T(8,128)(2,1)S(1)}, bf16[64,768]{1,0:T(8,128)(2,1)}, u32[]{:S(2)}) %copy-start.7) | copy-done | bytes 98328
  34.3 0.0 copy-start.8
  34.3 0.7 %copy-done.8 = s32[512]{0:T(512)S(1)} copy-done((s32[512]{0:T(512)S(1)}, s32[512]{0:T(512)}, u32[]{:S(2)}) %copy-start.8) | copy-done | bytes 2072
  35.0 1.2 %queries.1 = (bf16[64,1536]{1,0:T(8,128)(2,1)S(1)}, bf16[512,192]{1,0:T(8,128)(2,1)S(1)}, bf16[64,768]{1,0:T(8,128)(2,1)S(1)}) custom-call(s32[16]{0:T(128)S(1)} %copy-done.9, bf16[64,768]{1,0:T(8,128)(2,1)S(1)} %copy-done.7, s32[1,512]{1,0:T(1,128)S(1)} %bitcast.3, bf16[768,1536]{1,0:T(8,128)(2,1)S(1)} %copy-done.2), custom_call_target="tpu_custom_call" | custom-call | tf_op jit(solution)/shard_map/queries/pallas_call | solution.py:359
  36.2 0.0 collective-permute-done.15.refs_6_
  36.2 0.0 copy-done
  36.2 0.0 copy-done.1
  36.2 0.0 copy-start.3
  36.2 0.0 copy-start.4
  36.3 0.0 copy-start.5
  36.3 0.0 copy-start.6
  36.3 2.5 %shard_map.158 = (f32[1024,128]{1,0:T(8,128)S(1)}, f32[1024,256]{1,0:T(8,128)S(1)}) custom-call(bf16[64,768]{1,0:T(8,128)(2,1)S(1)} %get-tuple-element.22.refs_0_, bf16[64,768]{1,0:T(8,128)(2,1)S(1)} %collective-permute-done.11.refs_1_, bf16[64,768]{1,0:T(8,128)(2,1)S(1)} %collective-permute-done.12.refs_2_, ...), custom_call_target="tpu_custom_call" | custom-call | tf_op jit(solution)/shard_map/pallas_call | solution.py:390
  38.8 0.0 collective-permute-done.7.refs_4_
  38.8 0.0 collective-permute-done.10.refs_7_
  38.8 0.0 collective-permute-done.8.refs_5_
  38.8 0.0 collective-permute-done.9.refs_6_
  38.9 0.0 copy-done.3
  38.9 0.0 copy-done.4
  38.9 0.0 copy-done.5
  38.9 0.0 copy-done.6
  38.9 4.3 %shard_map.159 = (bf16[512,128]{1,0:T(8,128)(2,1)}, bf16[64,768]{1,0:T(8,128)(2,1)}) custom-call(bf16[64,768]{1,0:T(8,128)(2,1)S(1)} %collective-permute-done.2.refs_0_, bf16[64,768]{1,0:T(8,128)(2,1)S(1)} %collective-permute-done.4.refs_1_, bf16[64,768]{1,0:T(8,128)(2,1)S(1)} %collective-permute-done.5.refs_2_, ...), custom_call_target="tpu_custom_call" | custom-call | tf_op jit(solution)/shard_map/pallas_call | solution.py:390
Async XLA Ops:
  0.6 31.2 %copy-start.9 = (s32[16]{0:T(128)S(1)}, s32[16]{0:T(128)}, u32[]{:S(2)}) copy-start(s32[16]{0:T(128)} %info.5) | copy-start | bytes 196
  0.6 4.6 %collective-permute-start = (bf16[512,128]{1,0:T(8,128)(2,1)}, bf16[512,128]{1,0:T(8,128)(2,1)S(1)}, u32[]{:S(2)}, u32[]{:S(2)}) collective-permute-start(bf16[512,128]{1,0:T(8,128)(2,1)} %x.3), channel_id=1, source_target_pairs={{0,1},{1,0},{2,3},{3,2},{4,5},{5,4},{6,7},{7,6},{8,9},{9,8},{10,11... | collective-permute-start | bytes 393224 | tf_op jit(solution)/shard_map/ppermute | solution.py:311
  1.2 4.1 %collective-permute-start.1 = (bf16[512,128]{1,0:T(8,128)(2,1)}, bf16[512,128]{1,0:T(8,128)(2,1)S(1)}, u32[]{:S(2)}, u32[]{:S(2)}) collective-permute-start(bf16[512,128]{1,0:T(8,128)(2,1)} %x.3), channel_id=1, source_target_pairs={{1,2},{2,1},{3,4},{4,3},{5,6},{6,5},{7,8},{8,7},{9,10},{10,9},{11,... | collective-permute-start | bytes 393224 | tf_op jit(solution)/shard_map/ppermute | solution.py:321
  1.9 34.4 %copy-start = (bf16[768,1536]{1,0:T(8,128)(2,1)S(1)}, bf16[768,1536]{1,0:T(8,128)(2,1)}, u32[]{:S(2)}) copy-start(bf16[768,1536]{1,0:T(8,128)(2,1)} %refs_9_.3) | copy-start | bytes 7077892
  1.9 34.4 %copy-start.1 = (bf16[16,64,1024]{2,1,0:T(8,128)(2,1)S(1)}, bf16[16,64,1024]{2,1,0:T(8,128)(2,1)}, u32[]{:S(2)}) copy-start(bf16[16,64,1024]{2,1,0:T(8,128)(2,1)} %refs_10_.3) | copy-start | bytes 6291460
  5.3 0.7 %copy-start.10 = (bf16[512,128]{1,0:T(8,128)(2,1)}, bf16[512,128]{1,0:T(8,128)(2,1)S(1)}, u32[]{:S(2)}) copy-start(bf16[512,128]{1,0:T(8,128)(2,1)S(1)} %collective-permute-done.near) | copy-start | bytes 393220
  5.3 0.7 %copy-start.11 = (bf16[512,128]{1,0:T(8,128)(2,1)}, bf16[512,128]{1,0:T(8,128)(2,1)S(1)}, u32[]{:S(2)}) copy-start(bf16[512,128]{1,0:T(8,128)(2,1)S(1)} %collective-permute-done.1.far) | copy-start | bytes 393220
  10.0 12.8 %collective-permute-start.3 = (bf16[64,768]{1,0:T(8,128)(2,1)}, bf16[64,768]{1,0:T(8,128)(2,1)S(1)}, u32[]{:S(2)}, u32[]{:S(2)}) collective-permute-start(bf16[64,768]{1,0:T(8,128)(2,1)} %get-tuple-element.20.normed), channel_id=1, source_target_pairs={{0,8},{1,9},{2,10},{3,11},{4,12},{5,13},{6,14},{7,15},{8,0},{9,1},... | collective-permute-start | bytes 294920 | tf_op jit(solution)/shard_map/ppermute | solution.py:311
  17.0 5.9 %collective-permute-start.11 = (bf16[64,768]{1,0:T(8,128)(2,1)}, bf16[64,768]{1,0:T(8,128)(2,1)S(1)}, u32[]{:S(2)}, u32[]{:S(2)}) collective-permute-start(bf16[64,768]{1,0:T(8,128)(2,1)} %get-tuple-element.20.normed), channel_id=1, source_target_pairs={{0,2},{1,3},{2,0},{3,1},{4,6},{5,7},{6,4},{7,5},{8,10},{9,11},{10,... | collective-permute-start | bytes 294920 | tf_op jit(solution)/shard_map/ppermute | solution.py:311
  17.7 6.6 %collective-permute-start.12 = (bf16[64,768]{1,0:T(8,128)(2,1)}, bf16[64,768]{1,0:T(8,128)(2,1)S(1)}, u32[]{:S(2)}, u32[]{:S(2)}) collective-permute-start(bf16[64,768]{1,0:T(8,128)(2,1)} %get-tuple-element.20.normed), channel_id=1, source_target_pairs={{0,4},{1,5},{2,6},{3,7},{4,0},{5,1},{6,2},{7,3},{8,12},{9,13},{10,... | collective-permute-start | bytes 294920 | tf_op jit(solution)/shard_map/ppermute | solution.py:311
  19.2 6.6 %collective-permute-start.13 = (bf16[64,768]{1,0:T(8,128)(2,1)}, bf16[64,768]{1,0:T(8,128)(2,1)S(1)}, u32[]{:S(2)}, u32[]{:S(2)}) collective-permute-start(bf16[64,768]{1,0:T(8,128)(2,1)} %get-tuple-element.20.normed), channel_id=1, source_target_pairs={{0,1},{1,0},{2,3},{3,2},{4,5},{5,4},{6,7},{7,6},{8,9},{9,8},{10,11... | collective-permute-start | bytes 294920 | tf_op jit(solution)/shard_map/ppermute | solution.py:311
  19.2 7.3 %collective-permute-start.2 = (bf16[64,768]{1,0:T(8,128)(2,1)}, bf16[64,768]{1,0:T(8,128)(2,1)S(1)}, u32[]{:S(2)}, u32[]{:S(2)}) collective-permute-start(bf16[64,768]{1,0:T(8,128)(2,1)} %get-tuple-element.20.normed), channel_id=1, source_target_pairs={{0,6},{1,7},{2,4},{3,5},{4,2},{5,3},{6,0},{7,1},{8,14},{9,15},{10,... | collective-permute-start | bytes 294920 | tf_op jit(solution)/shard_map/ppermute | solution.py:311
  22.8 5.0 %collective-permute-start.16 = (bf16[64,768]{1,0:T(8,128)(2,1)S(1)}, bf16[64,768]{1,0:T(8,128)(2,1)S(1)}, u32[]{:S(2)}, u32[]{:S(2)}) collective-permute-start(bf16[64,768]{1,0:T(8,128)(2,1)S(1)} %collective-permute-done.3.refs_3_), channel_id=1, source_target_pairs={{0,1},{1,0},{2,3},{3,2},{4,5},{5,4},{6,7},{7,6},{8,9},{9,8},{10,11... | collective-permute-start | bytes 294920 | tf_op jit(solution)/shard_map/ppermute | solution.py:311
  22.8 5.0 %collective-permute-start.14 = (bf16[64,768]{1,0:T(8,128)(2,1)S(1)}, bf16[64,768]{1,0:T(8,128)(2,1)S(1)}, u32[]{:S(2)}, u32[]{:S(2)}) collective-permute-start(bf16[64,768]{1,0:T(8,128)(2,1)S(1)} %collective-permute-done.11.refs_1_), channel_id=1, source_target_pairs={{0,1},{1,0},{2,3},{3,2},{4,5},{5,4},{6,7},{7,6},{8,9},{9,8},{10,11... | collective-permute-start | bytes 294920 | tf_op jit(solution)/shard_map/ppermute | solution.py:311
  24.3 6.0 %collective-permute-start.6 = (bf16[64,768]{1,0:T(8,128)(2,1)S(1)}, bf16[64,768]{1,0:T(8,128)(2,1)S(1)}, u32[]{:S(2)}, u32[]{:S(2)}) collective-permute-start(bf16[64,768]{1,0:T(8,128)(2,1)S(1)} %collective-permute-done.3.refs_3_), channel_id=1, source_target_pairs={{0,6},{1,7},{2,4},{3,5},{4,2},{5,3},{6,0},{7,1},{8,14},{9,15},{10,... | collective-permute-start | bytes 294920 | tf_op jit(solution)/shard_map/ppermute | solution.py:311
  25.9 5.4 %collective-permute-start.4 = (bf16[64,768]{1,0:T(8,128)(2,1)S(1)}, bf16[64,768]{1,0:T(8,128)(2,1)S(1)}, u32[]{:S(2)}, u32[]{:S(2)}) collective-permute-start(bf16[64,768]{1,0:T(8,128)(2,1)S(1)} %collective-permute-done.3.refs_3_), channel_id=1, source_target_pairs={{0,2},{1,3},{2,0},{3,1},{4,6},{5,7},{6,4},{7,5},{8,10},{9,11},{10,... | collective-permute-start | bytes 294920 | tf_op jit(solution)/shard_map/ppermute | solution.py:311
  26.6 5.2 %collective-permute-start.5 = (bf16[64,768]{1,0:T(8,128)(2,1)S(1)}, bf16[64,768]{1,0:T(8,128)(2,1)S(1)}, u32[]{:S(2)}, u32[]{:S(2)}) collective-permute-start(bf16[64,768]{1,0:T(8,128)(2,1)S(1)} %collective-permute-done.3.refs_3_), channel_id=1, source_target_pairs={{0,4},{1,5},{2,6},{3,7},{4,0},{5,1},{6,2},{7,3},{8,12},{9,13},{10,... | collective-permute-start | bytes 294920 | tf_op jit(solution)/shard_map/ppermute | solution.py:311
  27.8 8.4 %collective-permute-start.15 = (bf16[64,768]{1,0:T(8,128)(2,1)S(1)}, bf16[64,768]{1,0:T(8,128)(2,1)S(1)}, u32[]{:S(2)}, u32[]{:S(2)}) collective-permute-start(bf16[64,768]{1,0:T(8,128)(2,1)S(1)} %collective-permute-done.12.refs_2_), channel_id=1, source_target_pairs={{0,1},{1,0},{2,3},{3,2},{4,5},{5,4},{6,7},{7,6},{8,9},{9,8},{10,11... | collective-permute-start | bytes 294920 | tf_op jit(solution)/shard_map/ppermute | solution.py:311
  27.8 11.0 %collective-permute-start.7 = (bf16[64,768]{1,0:T(8,128)(2,1)S(1)}, bf16[64,768]{1,0:T(8,128)(2,1)S(1)}, u32[]{:S(2)}, u32[]{:S(2)}) collective-permute-start(bf16[64,768]{1,0:T(8,128)(2,1)S(1)} %collective-permute-done.2.refs_0_), channel_id=1, source_target_pairs={{0,1},{1,0},{2,3},{3,2},{4,5},{5,4},{6,7},{7,6},{8,9},{9,8},{10,11... | collective-permute-start | bytes 294920 | tf_op jit(solution)/shard_map/ppermute | solution.py:311
  30.3 8.5 %collective-permute-start.10 = (bf16[64,768]{1,0:T(8,128)(2,1)S(1)}, bf16[64,768]{1,0:T(8,128)(2,1)S(1)}, u32[]{:S(2)}, u32[]{:S(2)}) collective-permute-start(bf16[64,768]{1,0:T(8,128)(2,1)S(1)} %collective-permute-done.6.refs_3_), channel_id=1, source_target_pairs={{0,1},{1,0},{2,3},{3,2},{4,5},{5,4},{6,7},{7,6},{8,9},{9,8},{10,11... | collective-permute-start | bytes 294920 | tf_op jit(solution)/shard_map/ppermute | solution.py:311
  31.2 7.6 %collective-permute-start.8 = (bf16[64,768]{1,0:T(8,128)(2,1)S(1)}, bf16[64,768]{1,0:T(8,128)(2,1)S(1)}, u32[]{:S(2)}, u32[]{:S(2)}) collective-permute-start(bf16[64,768]{1,0:T(8,128)(2,1)S(1)} %collective-permute-done.4.refs_1_), channel_id=1, source_target_pairs={{0,1},{1,0},{2,3},{3,2},{4,5},{5,4},{6,7},{7,6},{8,9},{9,8},{10,11... | collective-permute-start | bytes 294920 | tf_op jit(solution)/shard_map/ppermute | solution.py:311
  31.8 7.1 %collective-permute-start.9 = (bf16[64,768]{1,0:T(8,128)(2,1)S(1)}, bf16[64,768]{1,0:T(8,128)(2,1)S(1)}, u32[]{:S(2)}, u32[]{:S(2)}) collective-permute-start(bf16[64,768]{1,0:T(8,128)(2,1)S(1)} %collective-permute-done.5.refs_2_), channel_id=1, source_target_pairs={{0,1},{1,0},{2,3},{3,2},{4,5},{5,4},{6,7},{7,6},{8,9},{9,8},{10,11... | collective-permute-start | bytes 294920 | tf_op jit(solution)/shard_map/ppermute | solution.py:311
  31.8 1.7 %copy-start.2 = (bf16[768,1536]{1,0:T(8,128)(2,1)S(1)}, bf16[768,1536]{1,0:T(8,128)(2,1)}, u32[]{:S(2)}) copy-start(bf16[768,1536]{1,0:T(8,128)(2,1)} %qg.1) | copy-start | bytes 7077892
  33.4 0.9 %copy-start.7 = (bf16[64,768]{1,0:T(8,128)(2,1)S(1)}, bf16[64,768]{1,0:T(8,128)(2,1)}, u32[]{:S(2)}) copy-start(bf16[64,768]{1,0:T(8,128)(2,1)} %get-tuple-element.20.normed) | copy-start | bytes 294916
  34.3 0.7 %copy-start.8 = (s32[512]{0:T(512)S(1)}, s32[512]{0:T(512)}, u32[]{:S(2)}) copy-start(s32[512]{0:T(512)} %param.17) | copy-start | bytes 6148
  36.2 2.6 %copy-start.3 = (bf16[768,768]{1,0:T(8,128)(2,1)S(1)}, bf16[768,768]{1,0:T(8,128)(2,1)}, u32[]{:S(2)}) copy-start(bf16[768,768]{1,0:T(8,128)(2,1)} %refs_16_.1) | copy-start | bytes 3538948
  36.2 2.6 %copy-start.4 = (bf16[768,128]{1,0:T(8,128)(2,1)S(1)}, bf16[768,128]{1,0:T(8,128)(2,1)}, u32[]{:S(2)}) copy-start(bf16[768,128]{1,0:T(8,128)(2,1)} %refs_17_.1) | copy-start | bytes 589828
  36.3 2.6 %copy-start.5 = (f32[64,768]{1,0:T(8,128)S(1)}, f32[64,768]{1,0:T(8,128)}, u32[]{:S(2)}) copy-start(f32[64,768]{1,0:T(8,128)} %get-tuple-element.25.refs_13_) | copy-start | bytes 589828
  36.3 2.6 %copy-start.6 = (bf16[512,128]{1,0:T(8,128)(2,1)S(1)}, bf16[512,128]{1,0:T(8,128)(2,1)}, u32[]{:S(2)}) copy-start(bf16[512,128]{1,0:T(8,128)(2,1)} %get-tuple-element.26.refs_14_) | copy-start | bytes 393220
